TPU v7x, 32 devices: a whole 2x2x4 slice. The times are simulated.
32 devices in a mesh: end: 2 (over x), slab: 16 (over z, y, core).
Axes of the slice: x: 2, y: 2, z: 4, core: 2. Of those that a mesh axis runs over, the one named last changes fastest.
Arguments:
- w_field: float32 [128, 128, 256], P('slab'), may hold values from -4 to 4
- psi_init: float32 [128, 128, 256], P('slab'), may hold values from -3 to 3
- start_field: float32 [2, 128, 128, 256], P('end', 'slab'), may hold values from 0.25 to 8, as said below
- charges: int32 [5], replicated, may hold values from -1 to 1
Outputs:
- density: float32 [128, 128, 256], P('slab', 'end')
- potential: float32 [128, 128, 256], P('slab', 'end')
Inputs may be any that keep to these rules, and one draw needn't show every extreme that they name: `start_field`: positive entries.
All inputs are finite; a program needn't handle non-finite values.
Results may differ from a plain program's by a relative error of at most 0.0003.
The roundings to bfloat16 on the way count: a program that leaves them out, or rounds other values in their place, can miss the bound.
Values may be sent and summed in bfloat16 or wider, within the bound.
A program may use at most 64 MiB of HBM per device.

v0:
```python
import functools

import jax
import jax.numpy as jnp
from jax import lax
from jax.experimental import pallas as pl
from jax.experimental.pallas import tpu as pltpu
from jax.sharding import PartitionSpec as P

NS = 4
PAD = 8
mobility = 0.15
screening = 1.0
OWN, FOREIGN = 0, 1
MESH = pl.DeviceIdType.MESH


def kernel(ends, slabs, charges_ref, w_hbm, psi_hbm, start_hbm, density_ref, potential_ref,
           w_v, psi_v, start_v, factor, u, rounded, phi, rho, base, relaxed, sums,
           gate, local_sem, field_send, field_recv, psi_send, psi_recv, halo_send, halo_recv,
           rho_send, rho_recv, sum_send, sum_recv):
    side, slab = lax.axis_index("end"), lax.axis_index("slab")
    other = lax.rem(side + 1, ends)
    left = (side, lax.rem(slab + slabs - 1, slabs))
    right = (side, lax.rem(slab + 1, slabs))
    partner = (other, slab)
    layers, rows = w_hbm.shape[0], w_hbm.shape[1]
    half = rows // ends
    devices = ends * slabs
    flat = side * slabs + slab
    delta = 1.0 / NS

    def device(step):
        target = lax.rem(flat + step, devices)
        return (target // slabs, lax.rem(target, slabs))

    barrier = pltpu.get_barrier_semaphore()

    near = []
    width = 1
    while width < slabs:
        near.append((side, slab + width - 2 * width * lax.rem(slab // width, 2)))
        width *= 2
    near.append(partner)
    for neighbour in near:
        pl.semaphore_signal(barrier, inc=1, device_id=neighbour, device_id_type=MESH)

    def pieces(which):
        first = which * half
        return (
            (pl.multiple_of(first, 8), PAD, half),
            (pl.multiple_of(lax.rem(first + rows - PAD, rows), 8), 0, PAD),
            (pl.multiple_of(lax.rem(first + half, rows), 8), PAD + half, PAD),
        )

    mine, theirs = pieces(side), pieces(other)
    local = []
    for k, (source, target, first) in enumerate(
        ((w_hbm, w_v, 0), (psi_hbm, psi_v, 2), (start_hbm.at[0], start_v.at[OWN], 0))
    ):
        for n, (begin, at, count) in enumerate(mine):
            local.append(
                pltpu.make_async_copy(
                    source.at[:, pl.ds(begin, count)],
                    target.at[pl.ds(first, layers), pl.ds(at, count)],
                    local_sem.at[k, n],
                )
            )
    for copy in local:
        copy.start()

    q = [charges_ref[side * (NS - 2 * t) + t].astype(jnp.float32) for t in range(NS + 1)]
    pair = [0.5 * (q[k] + q[k + 1]) for k in range(NS)]

    def make_factor(x, carry):
        w, psi = w_v[x], psi_v[x + 2]
        for k in range(NS):
            factor[k, x] = jnp.exp(-0.5 * delta * (w + pair[k] * psi))
        return carry

    def index(chain, t):
        return t if chain == OWN else NS - 1 - t

    def begin_chain(chain, x):
        value = start_v[chain, x]
        rounded[chain, 0, x] = value.astype(jnp.bfloat16).astype(jnp.float32)
        u[chain, 0, x + 1] = factor[index(chain, 0), x] * value

    def around(value, axis):
        return pltpu.roll(value, 1, axis) + pltpu.roll(value, value.shape[axis] - 1, axis)

    def advanced(chain, t, x):
        center = u[chain, t, x + 1]
        total = u[chain, t, x] + u[chain, t, x + 2] + around(center, 0) + around(center, 1)
        return factor[index(chain, t), x] * (center + mobility * (total - 6.0 * center))

    def advance(chain, t, x):
        value = advanced(chain, t, x)
        rounded[chain, t + 1, x] = value.astype(jnp.bfloat16).astype(jnp.float32)
        if t + 1 < NS:
            u[chain, t + 1, x + 1] = factor[index(chain, t + 1), x] * value

    def loop(low, high, step):
        def body(x, carry):
            step(x)
            return carry

        lax.fori_loop(low, high, body, 0)

    def both(step):
        step(0)
        step(layers - 1)

    def halo(chain, t):
        return (
            pltpu.make_async_remote_copy(
                u.at[chain, t, 1], u.at[chain, t, layers + 1],
                halo_send.at[chain, t, 0], halo_recv.at[chain, t, 0],
                device_id=left, device_id_type=MESH,
            ),
            pltpu.make_async_remote_copy(
                u.at[chain, t, layers], u.at[chain, t, 0],
                halo_send.at[chain, t, 1], halo_recv.at[chain, t, 1],
                device_id=right, device_id_type=MESH,
            ),
        )

    sent = []

    def send_halo(chain, t):
        for copy in halo(chain, t):
            copy.start()
            sent.append(copy)

    def wait_halo(chain, t):
        for copy in halo(chain, t):
            copy.wait_recv()

    groups = [(0, layers - 1), (1, layers - 2), (2, layers - 3), tuple(range(3, layers - 3))]
    order = [x for group in groups for x in group]

    def field(x):
        return [
            pltpu.make_async_remote_copy(
                start_hbm.at[0, x, pl.ds(begin, count)],
                start_v.at[FOREIGN, x, pl.ds(at, count)],
                field_send.at[x, n], field_recv.at[x, n],
                device_id=partner, device_id_type=MESH,
            )
            for n, (begin, at, count) in enumerate(theirs)
        ]

    def arrive(group):
        for x in groups[group]:
            for copy in field(x):
                copy.wait_recv()
        for x in groups[group]:
            begin_chain(FOREIGN, x)

    def psi_halo():
        copies = []
        for n, (begin, at, count) in enumerate(mine):
            deep = 2 if count == half else 1
            copies.append(
                pltpu.make_async_remote_copy(
                    psi_hbm.at[pl.ds(0, deep), pl.ds(begin, count)],
                    psi_v.at[pl.ds(layers + 2, deep), pl.ds(at, count)],
                    psi_send.at[0, n], psi_recv.at[0, n],
                    device_id=left, device_id_type=MESH,
                )
            )
            copies.append(
                pltpu.make_async_remote_copy(
                    psi_hbm.at[pl.ds(layers - deep, deep), pl.ds(begin, count)],
                    psi_v.at[pl.ds(2 - deep, deep), pl.ds(at, count)],
                    psi_send.at[1, n], psi_recv.at[1, n],
                    device_id=right, device_id_type=MESH,
                )
            )
        return copies

    pl.semaphore_wait(barrier, len(near))
    for x in order:
        for copy in field(x):
            copy.start()
            sent.append(copy)
    for copy in local:
        copy.wait()
    stages = len(near)
    for stage, neighbour in enumerate(near):
        pl.semaphore_signal(gate.at[stage], inc=1, device_id=neighbour, device_id_type=MESH)
        low, high = layers * stage // stages, layers * (stage + 1) // stages
        lax.fori_loop(low, high, make_factor, 0)
        loop(low, high, functools.partial(begin_chain, OWN))
        if neighbour is not partner:
            pl.semaphore_wait(gate.at[stage], 1)
    send_halo(OWN, 0)
    loop(1, layers - 1, functools.partial(advance, OWN, 0))

    def make_base(x):
        center = psi_v[x + 1]
        total = psi_v[x] + psi_v[x + 2] + around(center, 0) + around(center, 1)
        base[x] = total - ion_charge(center) + screening * center

    loop(2, layers, make_base)

    arrive(0)
    send_halo(FOREIGN, 0)
    wait_halo(OWN, 0)
    both(functools.partial(advance, OWN, 0))
    send_halo(OWN, 1)
    loop(1, layers - 1, functools.partial(advance, OWN, 1))

    arrive(1)
    wait_halo(FOREIGN, 0)
    both(functools.partial(advance, FOREIGN, 0))
    send_halo(FOREIGN, 1)
    wait_halo(OWN, 1)
    both(functools.partial(advance, OWN, 1))
    send_halo(OWN, 2)
    loop(1, layers - 1, functools.partial(advance, OWN, 2))

    arrive(2)
    for x in (1, layers - 2):
        advance(FOREIGN, 0, x)
    wait_halo(FOREIGN, 1)
    both(functools.partial(advance, FOREIGN, 1))
    send_halo(FOREIGN, 2)
    wait_halo(OWN, 2)
    both(functools.partial(advance, OWN, 2))
    send_halo(OWN, 3)
    loop(1, layers - 1, functools.partial(advance, OWN, 3))

    arrive(3)
    for x in (2, layers - 3):
        advance(FOREIGN, 0, x)
    for x in (1, layers - 2):
        advance(FOREIGN, 1, x)
    wait_halo(FOREIGN, 2)
    both(functools.partial(advance, FOREIGN, 2))
    send_halo(FOREIGN, 3)
    psi_copies = psi_halo()
    for copy in psi_copies:
        copy.start()
        sent.append(copy)
    loop(3, layers - 3, functools.partial(advance, FOREIGN, 0))
    loop(2, layers - 2, functools.partial(advance, FOREIGN, 1))
    loop(1, layers - 1, functools.partial(advance, FOREIGN, 2))
    wait_halo(OWN, 3)
    both(functools.partial(advance, OWN, 3))

    weights = [delta * (0.5 if t in (0, NS) else 1.0) for t in range(NS + 1)]
    charged = [weights[t] * q[t] for t in range(NS + 1)]

    def gathered(x):
        phi_layer, rho_layer = 0.0, 0.0
        for t in range(1, NS + 1):
            product = rounded[OWN, t, x] * rounded[FOREIGN, NS - t, x]
            phi_layer = phi_layer + weights[t] * product
            rho_layer = rho_layer + charged[t] * product
        return phi_layer, rho_layer

    def gather(x):
        phi[x], rho[x + 1] = gathered(x)

    def last_product(x):
        value = advanced(FOREIGN, NS - 1, x).astype(jnp.bfloat16).astype(jnp.float32)
        return rounded[OWN, 0, x] * value

    def finish(x):
        product = last_product(x)
        phi[x] += weights[0] * product
        rho[x + 1] += charged[0] * product

    def whole(x):
        phi_layer, rho_layer = gathered(x)
        product = last_product(x)
        phi[x] = phi_layer + weights[0] * product
        rho[x + 1] = rho_layer + charged[0] * product

    both(gather)
    loop(1, layers - 1, whole)

    inner = pl.ds(PAD, half)

    def add(x, carry):
        return carry + phi[x, inner]

    partial = lax.fori_loop(2, layers - 1, add, phi[1, inner])
    wait_halo(FOREIGN, NS - 1)
    both(finish)
    rho_copies = (
        pltpu.make_async_remote_copy(
            rho.at[1, inner], rho.at[layers + 1, inner], rho_send.at[0], rho_recv.at[0],
            device_id=left, device_id_type=MESH,
        ),
        pltpu.make_async_remote_copy(
            rho.at[layers, inner], rho.at[0, inner], rho_send.at[1], rho_recv.at[1],
            device_id=right, device_id_type=MESH,
        ),
    )
    partial = partial + phi[0, inner] + phi[layers - 1, inner]
    sums[0] = jnp.sum(
        sum(partial[:, k:k + 128] for k in range(0, partial.shape[1], 128)), axis=0, keepdims=True
    )

    def share(step, carry):
        pltpu.make_async_remote_copy(
            sums.at[0], sums.at[step], sum_send, sum_recv,
            device_id=device(step), device_id_type=MESH,
        ).start()
        return carry

    pl.semaphore_wait(gate.at[stages - 1], 1)
    lax.fori_loop(1, devices, share, 0)
    for copy in rho_copies:
        copy.start()
        sent.append(copy)

    for copy in psi_copies:
        copy.wait_recv()

    for x in (0, 1, layers, layers + 1):
        make_base(x)

    others = sums.at[pl.ds(1, devices - 1)]
    pltpu.make_async_copy(others, others, sum_recv).wait()
    cells = float(devices * layers * half * w_hbm.shape[2])
    inverse = cells / jnp.sum(sums[...])

    def relax_once(x):
        relaxed[x] = (base[x] + rho[x] * inverse) * (1.0 / (6.0 + screening))

    def first(x):
        density_ref[x] = phi[x, inner] * inverse
        relax_once(x + 1)

    loop(0, layers, first)

    def second(x):
        center = relaxed[x + 1]
        total = relaxed[x] + relaxed[x + 2] + around(center, 0) + around(center, 1)
        value = total + rho[x + 1] * inverse - ion_charge(center) + screening * center
        potential_ref[x] = value[PAD:PAD + half] * (1.0 / (6.0 + screening))

    loop(1, layers - 1, second)
    for copy in rho_copies:
        copy.wait_recv()
    relax_once(0)
    relax_once(layers + 1)
    both(second)

    for copy in sent:
        copy.wait_send()
    pltpu.make_async_copy(others, others, sum_send).wait()


def ion_charge(value):
    return (2.0 * screening) * jnp.tanh(0.5 * value)


def body(ends, slabs, w_field, psi_init, start_field, charges):
    layers, rows, depth = w_field.shape
    half = rows // ends
    wide = half + 2 * PAD
    devices = ends * slabs
    stages = slabs.bit_length()
    out = jax.ShapeDtypeStruct((layers, half, depth), jnp.float32)
    dma = pltpu.SemaphoreType.DMA

    def tile(*lead):
        return pltpu.VMEM((*lead, wide, depth), jnp.float32)

    hbm = pl.BlockSpec(memory_space=pltpu.HBM)
    vmem = pl.BlockSpec(memory_space=pltpu.VMEM)
    return pl.pallas_call(
        functools.partial(kernel, ends, slabs),
        out_shape=(out, out),
        in_specs=[pl.BlockSpec(memory_space=pltpu.SMEM), hbm, hbm, hbm],
        out_specs=(vmem, vmem),
        scratch_shapes=[
            tile(layers), tile(layers + 4), tile(2, layers), tile(NS, layers),
            tile(2, NS, layers + 2), tile(2, NS + 1, layers), tile(layers), tile(layers + 2),
            tile(layers + 2), tile(layers + 2), pltpu.VMEM((devices, 1, 128), jnp.float32),
            pltpu.SemaphoreType.REGULAR((stages,)), dma((3, 3)), dma((layers, 3)), dma((layers, 3)), dma((2, 3)), dma((2, 3)),
            dma((2, NS, 2)), dma((2, NS, 2)), dma((2,)), dma((2,)), dma(()), dma(()),
        ],
        compiler_params=pltpu.CompilerParams(
            collective_id=0, has_side_effects=True, vmem_limit_bytes=30 * 1024 * 1024
        ),
        name="scf_step",
    )(charges, *[pltpu.with_memory_space_constraint(v, pltpu.HBM) for v in (w_field, psi_init, start_field)])


def solution(mesh):
    in_specs = (P("slab", None, None), P("slab", None, None), P("end", "slab", None, None), P())
    out_specs = (P("slab", "end", None), P("slab", "end", None))
    step = functools.partial(body, mesh.shape["end"], mesh.shape["slab"])
    return jax.shard_map(step, mesh=mesh, in_specs=in_specs, out_specs=out_specs, check_vma=False)
```

profile of v0, /device:TPU:0, one launch (start us, length us, event | category | flops | bytes accessed | tf_op | source)
XLA Modules:
  0.0 38.8 jit_solution(11590226411625054319)
XLA Ops:
  0.6 0.0 copy-start
  0.6 0.6 %copy-done = s32[5]{0:T(128)S(1)} copy-done((s32[5]{0:T(128)S(1)}, s32[5]{0:T(128)}, u32[]{:S(2)}) %copy-start) | copy-done | bytes 44
  1.3 35.9 %scf_step.1 = (f32[8,64,256]{2,1,0:T(8,128)S(1)}, f32[8,64,256]{2,1,0:T(8,128)S(1)}) custom-call(s32[5]{0:T(128)S(1)} %copy-done, f32[8,128,256]{2,1,0:T(8,128)} %w_hbm.1, f32[8,128,256]{2,1,0:T(8,128)} %psi_hbm.1, f32[1,8,128,256]{3,2,1,0:T(8,128)} %start_hbm.1), custom_call_target="tpu_custom_call" | custom-call | tf_op jit(solution)/shard_map/scf_step/pallas_call | solution.py:376
  37.2 0.8 %copy.8 = f32[8,64,256]{2,1,0:T(8,128)} copy(f32[8,64,256]{2,1,0:T(8,128)S(1)} %get-tuple-element.4) | data formatting | bytes 1048576
  38.0 0.8 %copy.9 = f32[8,64,256]{2,1,0:T(8,128)} copy(f32[8,64,256]{2,1,0:T(8,128)S(1)} %get-tuple-element.5) | data formatting | bytes 1048576
Async XLA Ops:
  0.6 0.7 %copy-start = (s32[5]{0:T(128)S(1)}, s32[5]{0:T(128)}, u32[]{:S(2)}) copy-start(s32[5]{0:T(128)} %charges_ref.1) | copy-start | bytes 64
where the time goes:
time: 38.9 us; the launch traced here: 38.8 us
  Pallas kernels  35.9 us (92%)
  local copies, waits for them, and re-layouts  2.24 us (6%)
  between operations  0.65 us (2%)
    pallas_call x1, Pallas kernels, body(): pl.pallas_call(functools.partial(kernel, ends, slabs), out_shape=(out, ou...  35.9 us
    unnamed x4, local copies, waits for them, and re-layouts  2.24 us

commit v1 on v0

--- a/solution.py
+++ b/solution.py
@@ -15,8 +15,8 @@
 MESH = pl.DeviceIdType.MESH
 
 
-def kernel(ends, slabs, charges_ref, w_hbm, psi_hbm, start_hbm, density_ref, potential_ref,
-           w_v, psi_v, start_v, factor, u, rounded, phi, rho, base, relaxed, sums,
+def kernel(ends, slabs, charges_hbm, w_hbm, psi_hbm, start_hbm, density_ref, potential_ref,
+           charges_ref, charges_sem, w_v, psi_v, start_v, factor, u, rounded, phi, rho, base, relaxed, sums,
            gate, local_sem, field_send, field_recv, psi_send, psi_recv, halo_send, halo_recv,
            rho_send, rho_recv, sum_send, sum_recv):
     side, slab = lax.axis_index("end"), lax.axis_index("slab")
@@ -36,13 +36,16 @@
 
     barrier = pltpu.get_barrier_semaphore()
 
+    charges_copy = pltpu.make_async_copy(charges_hbm, charges_ref, charges_sem)
+    charges_copy.start()
+
     near = []
     width = 1
     while width < slabs:
         near.append((side, slab + width - 2 * width * lax.rem(slab // width, 2)))
         width *= 2
     near.append(partner)
-    for neighbour in near:
+    for neighbour in near + [left, right]:
         pl.semaphore_signal(barrier, inc=1, device_id=neighbour, device_id_type=MESH)
 
     def pieces(which):
@@ -69,6 +72,7 @@
     for copy in local:
         copy.start()
 
+    charges_copy.wait()
     q = [charges_ref[side * (NS - 2 * t) + t].astype(jnp.float32) for t in range(NS + 1)]
     pair = [0.5 * (q[k] + q[k + 1]) for k in range(NS)]
 
@@ -92,7 +96,7 @@
     def advanced(chain, t, x):
         center = u[chain, t, x + 1]
         total = u[chain, t, x] + u[chain, t, x + 2] + around(center, 0) + around(center, 1)
-        return factor[index(chain, t), x] * (center + mobility * (total - 6.0 * center))
+        return factor[index(chain, t), x] * ((1.0 - 6.0 * mobility) * center + mobility * total)
 
     def advance(chain, t, x):
         value = advanced(chain, t, x)
@@ -179,7 +183,7 @@
             )
         return copies
 
-    pl.semaphore_wait(barrier, len(near))
+    pl.semaphore_wait(barrier, len(near) + 2)
     for x in order:
         for copy in field(x):
             copy.start()
@@ -187,14 +191,23 @@
     for copy in local:
         copy.wait()
     stages = len(near)
-    for stage, neighbour in enumerate(near):
-        pl.semaphore_signal(gate.at[stage], inc=1, device_id=neighbour, device_id_type=MESH)
-        low, high = layers * stage // stages, layers * (stage + 1) // stages
-        lax.fori_loop(low, high, make_factor, 0)
-        loop(low, high, functools.partial(begin_chain, OWN))
-        if neighbour is not partner:
-            pl.semaphore_wait(gate.at[stage], 1)
+
+    def open_gate(stage):
+        pl.semaphore_signal(gate.at[stage], inc=1, device_id=near[stage], device_id_type=MESH)
+
+    def pass_gate(stage):
+        pl.semaphore_wait(gate.at[stage], 1)
+        if stage + 1 < stages:
+            open_gate(stage + 1)
+
+    open_gate(0)
+    for x in (0, layers - 1):
+        make_factor(x, 0)
+        begin_chain(OWN, x)
     send_halo(OWN, 0)
+    pass_gate(0)
+    lax.fori_loop(1, layers - 1, make_factor, 0)
+    loop(1, layers - 1, functools.partial(begin_chain, OWN))
     loop(1, layers - 1, functools.partial(advance, OWN, 0))
 
     def make_base(x):
@@ -204,6 +217,7 @@
 
     loop(2, layers, make_base)
 
+    pass_gate(1)
     arrive(0)
     send_halo(FOREIGN, 0)
     wait_halo(OWN, 0)
@@ -211,6 +225,7 @@
     send_halo(OWN, 1)
     loop(1, layers - 1, functools.partial(advance, OWN, 1))
 
+    pass_gate(2)
     arrive(1)
     wait_halo(FOREIGN, 0)
     both(functools.partial(advance, FOREIGN, 0))
@@ -220,6 +235,7 @@
     send_halo(OWN, 2)
     loop(1, layers - 1, functools.partial(advance, OWN, 2))
 
+    pass_gate(3)
     arrive(2)
     for x in (1, layers - 2):
         advance(FOREIGN, 0, x)
@@ -231,6 +247,8 @@
     send_halo(OWN, 3)
     loop(1, layers - 1, functools.partial(advance, OWN, 3))
 
+    for stage in range(4, stages):
+        pass_gate(stage)
     arrive(3)
     for x in (2, layers - 3):
         advance(FOREIGN, 0, x)
@@ -311,7 +329,6 @@
         ).start()
         return carry
 
-    pl.semaphore_wait(gate.at[stages - 1], 1)
     lax.fori_loop(1, devices, share, 0)
     for copy in rho_copies:
         copy.start()
@@ -376,10 +393,10 @@
     return pl.pallas_call(
         functools.partial(kernel, ends, slabs),
         out_shape=(out, out),
-        in_specs=[pl.BlockSpec(memory_space=pltpu.SMEM), hbm, hbm, hbm],
+        in_specs=[hbm, hbm, hbm, hbm],
         out_specs=(vmem, vmem),
         scratch_shapes=[
-            tile(layers), tile(layers + 4), tile(2, layers), tile(NS, layers),
+            pltpu.SMEM((NS + 1,), jnp.int32), dma(()), tile(layers), tile(layers + 4), tile(2, layers), tile(NS, layers),
             tile(2, NS, layers + 2), tile(2, NS + 1, layers), tile(layers), tile(layers + 2),
             tile(layers + 2), tile(layers + 2), pltpu.VMEM((devices, 1, 128), jnp.float32),
             pltpu.SemaphoreType.REGULAR((stages,)), dma((3, 3)), dma((layers, 3)), dma((layers, 3)), dma((2, 3)), dma((2, 3)),
@@ -389,7 +406,7 @@
             collective_id=0, has_side_effects=True, vmem_limit_bytes=30 * 1024 * 1024
         ),
         name="scf_step",
-    )(charges, *[pltpu.with_memory_space_constraint(v, pltpu.HBM) for v in (w_field, psi_init, start_field)])
+    )(*[pltpu.with_memory_space_constraint(v, pltpu.HBM) for v in (charges, w_field, psi_init, start_field)])
 
 
 def solution(mesh):

time: 38.9 us -> 38.3 us (0.985)
  local copies, waits for them, and re-layouts: 2.24 us -> 1.59 us
    unnamed x4 -> x2, local copies, waits for them, and re-layouts: 2.24 us -> 1.59 us
where the time goes in v1:
time: 38.3 us; the launch traced here: 38.2 us
  Pallas kernels  35.9 us (94%)
  local copies, waits for them, and re-layouts  1.59 us (4%)
  between operations  0.64 us (2%)
    pallas_call x1, Pallas kernels, body(): pl.pallas_call(functools.partial(kernel, ends, slabs), out_shape=(out, ou...  35.9 us
    unnamed x2, local copies, waits for them, and re-layouts  1.59 us

profile of v1, /device:TPU:0, one launch (start us, length us, event | category | flops | bytes accessed | tf_op | source)
XLA Modules:
  0.0 38.2 jit_solution(12641746623006066999)
XLA Ops:
  0.6 35.9 %scf_step.1 = (f32[8,64,256]{2,1,0:T(8,128)S(1)}, f32[8,64,256]{2,1,0:T(8,128)S(1)}) custom-call(s32[5]{0:T(128)} %charges_hbm.1, f32[8,128,256]{2,1,0:T(8,128)} %w_hbm.1, f32[8,128,256]{2,1,0:T(8,128)} %psi_hbm.1, f32[1,8,128,256]{3,2,1,0:T(8,128)} %start_hbm.1), custom_call_target="tpu_custom_call" | custom-call | tf_op jit(solution)/shard_map/scf_step/pallas_call | solution.py:393
  36.6 0.8 %copy.8 = f32[8,64,256]{2,1,0:T(8,128)} copy(f32[8,64,256]{2,1,0:T(8,128)S(1)} %get-tuple-element.4) | data formatting | bytes 1048576
  37.4 0.8 %copy.9 = f32[8,64,256]{2,1,0:T(8,128)} copy(f32[8,64,256]{2,1,0:T(8,128)S(1)} %get-tuple-element.5) | data formatting | bytes 1048576

commit v2 on v1

v2 whole, which is shorter than its diff:
```python
import functools
import math

import jax
import jax.numpy as jnp
from jax import lax
from jax.experimental import pallas as pl
from jax.experimental.pallas import tpu as pltpu
from jax.sharding import PartitionSpec as P

NS = 4
PAD = 8
mobility = 0.15
screening = 1.0
OWN, FOREIGN = 0, 1
W_MAX, PSI_MAX = 4.0, 3.0
START_MIN, START_MAX = 0.25, 8.0
CODES, OFFSET = 65535.0, 32768
MARGIN = 0.001
MESH = pl.DeviceIdType.MESH


def kernel(ends, slabs, charges_hbm, w_hbm, psi_hbm, start_hbm, density_ref, potential_ref,
           charges_ref, w_v, psi_v, start_v, theirs_v, factor, u, rounded, phi, rho, base, relaxed, sums,
           field_out, field_in, edge_out, edge_in, halo_out, halo_in,
           gate, charges_sem, local_sem, field_send, field_recv, edge_send, edge_recv, halo_send, halo_recv,
           rho_send, rho_recv, sum_send, sum_recv):
    side, slab = lax.axis_index("end"), lax.axis_index("slab")
    other = lax.rem(side + 1, ends)
    left = (side, lax.rem(slab + slabs - 1, slabs))
    right = (side, lax.rem(slab + 1, slabs))
    partner = (other, slab)
    layers, rows = w_hbm.shape[0], w_hbm.shape[1]
    half = rows // ends
    devices = ends * slabs
    flat = side * slabs + slab
    delta = 1.0 / NS

    def device(step):
        target = lax.rem(flat + step, devices)
        return (target // slabs, lax.rem(target, slabs))

    barrier = pltpu.get_barrier_semaphore()
    charges_copy = pltpu.make_async_copy(charges_hbm, charges_ref, charges_sem)
    charges_copy.start()

    near = []
    width = 1
    while width < slabs:
        near.append((side, slab + width - 2 * width * lax.rem(slab // width, 2)))
        width *= 2
    near.append(partner)
    for neighbour in near + [left, right]:
        pl.semaphore_signal(barrier, inc=1, device_id=neighbour, device_id_type=MESH)

    def pieces(which):
        first = which * half
        return (
            (pl.multiple_of(first, 8), PAD, half),
            (pl.multiple_of(lax.rem(first + rows - PAD, rows), 8), 0, PAD),
            (pl.multiple_of(lax.rem(first + half, rows), 8), PAD + half, PAD),
        )

    mine, theirs = pieces(side), pieces(other)
    local = []
    for k, (source, target, first, parts) in enumerate((
        (start_hbm.at[0], theirs_v, 0, theirs), (w_hbm, w_v, 1, mine),
        (psi_hbm, psi_v, 2, mine), (start_hbm.at[0], start_v, 0, mine),
    )):
        local.append([
            pltpu.make_async_copy(
                source.at[:, pl.ds(begin, count)],
                target.at[pl.ds(first, layers), pl.ds(at, count)],
                local_sem.at[k, n],
            )
            for n, (begin, at, count) in enumerate(parts)
        ])
    for copies in local:
        for copy in copies:
            copy.start()

    def loop(low, high, step):
        def body(x, carry):
            step(x)
            return carry

        lax.fori_loop(low, high, body, 0)

    def span(t):
        reach = 0.5 * delta * (W_MAX + PSI_MAX) * t + MARGIN
        return math.log(START_MIN) - reach, math.log(START_MAX) + reach

    def write_code(value, low, high):
        scaled = value * (CODES / (high - low)) + (0.5 - low * (CODES / (high - low)))
        return (scaled.astype(jnp.int32) - OFFSET).astype(jnp.int16)

    def read_code(code, low, high):
        step = (high - low) / CODES
        return code.astype(jnp.int32).astype(jnp.float32) * step + (low + OFFSET * step)

    def write_log(value, t):
        return write_code(jnp.log(value), *span(t))

    def read_log(code, t):
        return jnp.exp(read_code(code, *span(t)))

    w_span, psi_span = (-W_MAX - MARGIN, W_MAX + MARGIN), (-PSI_MAX - MARGIN, PSI_MAX + MARGIN)

    for copy in local[0]:
        copy.wait()

    def code_field(x):
        field_out[x] = write_log(theirs_v[x], 0)

    loop(0, layers, code_field)

    charges_copy.wait()
    q = [charges_ref[side * (NS - 2 * t) + t].astype(jnp.float32) for t in range(NS + 1)]
    pair = [0.5 * (q[k] + q[k + 1]) for k in range(NS)]

    def make_factor(x):
        w, psi = w_v[x + 1], psi_v[x + 2]
        for k in range(NS):
            factor[k, x + 1] = jnp.exp(-0.5 * delta * (w + pair[k] * psi))

    def index(chain, t):
        return t if chain == OWN else NS - 1 - t

    def to_bfloat16(value):
        return value.astype(jnp.bfloat16).astype(jnp.float32)

    def begin_chain(chain, x):
        value = start_v[x] if chain == OWN else read_log(field_in[x], 0)
        rounded[chain, 0, x] = to_bfloat16(value)
        u[chain, 0, x + 2] = factor[index(chain, 0), x + 1] * value

    def around(value, axis):
        return pltpu.roll(value, 1, axis) + pltpu.roll(value, value.shape[axis] - 1, axis)

    def advanced(chain, t, x):
        center = u[chain, t, x + 2]
        total = u[chain, t, x + 1] + u[chain, t, x + 3] + around(center, 0) + around(center, 1)
        return factor[index(chain, t), x + 1] * ((1.0 - 6.0 * mobility) * center + mobility * total)

    def advance_halo(chain, t, x):
        u[chain, t + 1, x + 2] = factor[index(chain, t + 1), x + 1] * advanced(chain, t, x)

    def advance(chain, t, x):
        value = advanced(chain, t, x)
        rounded[chain, t + 1, x] = to_bfloat16(value)
        if t + 1 < NS:
            u[chain, t + 1, x + 2] = factor[index(chain, t + 1), x + 1] * value

    def adv(chain, t, low, high):
        loop(low, high, functools.partial(advance, chain, t))

    def outer(step):
        loop(0, 2, lambda k: step((layers - 1) * k))

    def beyond(step):
        loop(0, 2, lambda k: step((layers + 1) * k - 1))

    def edge_pair(d, step):
        loop(0, 2, lambda j: step(j + d * (layers - 2)))

    def out_layer(d, j):
        return layers - 1 - j if d else j

    def in_layer(d, j):
        return -1 - j if d else layers + j

    targets = (left, right)

    for copies in local[1:]:
        for copy in copies:
            copy.wait()
    loop(0, layers, make_factor)
    loop(0, layers, functools.partial(begin_chain, OWN))
    for d in (0, 1):
        def code_edge(j, d=d):
            x = out_layer(d, j)
            edge_out[d, j] = write_log(u[OWN, 0, x + 2], 1)
            edge_out[d, 3 + j] = write_code(psi_v[x + 2], *psi_span)

        loop(0, 2, code_edge)
        edge_out[d, 2] = write_code(w_v[out_layer(d, 0) + 1], *w_span)
    adv(OWN, 0, 1, layers - 1)
    adv(OWN, 1, 2, layers - 2)

    def make_base(x):
        center = psi_v[x + 2]
        total = psi_v[x + 1] + psi_v[x + 3] + around(center, 0) + around(center, 1)
        base[x + 1] = (total - ion_charge(center) + screening * center) * (1.0 / (6.0 + screening))

    groups = [(0, layers - 1), (1, layers - 2), (2, layers - 3), tuple(range(3, layers - 3))]
    order = [x for group in groups for x in group]
    sent = []

    def send(copy):
        copy.start()
        sent.append(copy)
        return copy

    pl.semaphore_wait(barrier, len(near) + 2)
    fields = {
        x: send(pltpu.make_async_remote_copy(
            field_out.at[x], field_in.at[x], field_send.at[x], field_recv.at[x],
            device_id=partner, device_id_type=MESH,
        ))
        for x in order
    }
    edges = [
        send(pltpu.make_async_remote_copy(
            edge_out.at[d, pl.ds(first, count)], edge_in.at[d, pl.ds(first, count)],
            edge_send.at[d, n], edge_recv.at[d, n], device_id=targets[d], device_id_type=MESH,
        ))
        for n, (first, count) in enumerate(((0, 4), (4, 1))) for d in (0, 1)
    ]

    def halo(kind, d, first, count):
        return pltpu.make_async_remote_copy(
            halo_out.at[kind, d, pl.ds(first, count)], halo_in.at[kind, d, pl.ds(first, count)],
            halo_send.at[kind, d, first], halo_recv.at[kind, d, first],
            device_id=targets[d], device_id_type=MESH,
        )

    stages = len(near)

    def open_gate(stage):
        pl.semaphore_signal(gate.at[stage], inc=1, device_id=near[stage], device_id_type=MESH)

    def pass_gate(stage):
        pl.semaphore_wait(gate.at[stage], 1)
        if stage + 1 < stages:
            open_gate(stage + 1)

    open_gate(0)
    adv(OWN, 2, 3, layers - 3)
    pass_gate(0)
    loop(1, layers - 1, make_base)
    pass_gate(1)

    def arrive(group):
        for x in groups[group]:
            fields[x].wait_recv()
        for x in groups[group]:
            begin_chain(FOREIGN, x)

    copies = []
    for j in (0, 1):
        arrive(j)
        for d in (0, 1):
            halo_out[0, d, j] = write_log(u[FOREIGN, 0, out_layer(d, j) + 2], 1)
            copies.append(send(halo(0, d, j, 1)))

    pass_gate(2)
    arrive(2)
    adv(FOREIGN, 0, 1, 2)
    adv(FOREIGN, 0, layers - 2, layers - 1)

    for copy in edges[:2]:
        copy.wait_recv()
    for d in (0, 1):
        x = in_layer(d, 0)
        w_v[x + 1] = read_code(edge_in[d, 2], *w_span)
        psi_v[x + 2] = read_code(edge_in[d, 3], *psi_span)
        for j in (0, 1):
            u[OWN, 0, in_layer(d, j) + 2] = read_log(edge_in[d, j], 1)
    beyond(make_factor)
    beyond(functools.partial(advance_halo, OWN, 0))
    outer(functools.partial(advance, OWN, 0))

    def half_way(chain, kind):
        result = []
        for d in (0, 1):
            edge_pair(d, functools.partial(advance, chain, 1))
            for j in (0, 1):
                halo_out[kind, d, j] = write_log(u[chain, 2, out_layer(d, j) + 2], 5)
            result.append(send(halo(kind, d, 0, 2)))
        return result

    own_copies = half_way(OWN, 1)

    pass_gate(3)
    arrive(3)
    adv(FOREIGN, 0, 2, layers - 2)
    adv(FOREIGN, 1, 2, layers - 2)
    for copy in copies:
        copy.wait_recv()
    for d in (0, 1):
        for j in (0, 1):
            u[FOREIGN, 0, in_layer(d, j) + 2] = read_log(halo_in[0, d, j], 1)
    beyond(functools.partial(advance_halo, FOREIGN, 0))
    outer(functools.partial(advance, FOREIGN, 0))
    foreign_copies = half_way(FOREIGN, 2)

    for stage in range(4, stages):
        pass_gate(stage)
    adv(OWN, 2, 1, 3)
    adv(OWN, 2, layers - 3, layers - 1)
    adv(OWN, 3, 2, layers - 2)
    adv(FOREIGN, 2, 1, layers - 1)

    def second_half(chain, kind, copies):
        for copy in copies:
            copy.wait_recv()
        for d in (0, 1):
            for j in (0, 1):
                u[chain, 2, in_layer(d, j) + 2] = read_log(halo_in[kind, d, j], 5)
        beyond(functools.partial(advance_halo, chain, 2))
        outer(functools.partial(advance, chain, 2))

    weights = [delta * (0.5 if t in (0, NS) else 1.0) for t in range(NS + 1)]
    charged = [weights[t] * q[t] for t in range(NS + 1)]

    def gathered(x):
        phi_layer, rho_layer = 0.0, 0.0
        for t in range(1, NS + 1):
            product = rounded[OWN, t, x] * rounded[FOREIGN, NS - t, x]
            phi_layer = phi_layer + weights[t] * product
            rho_layer = rho_layer + charged[t] * product
        return phi_layer, rho_layer

    def whole(x):
        phi_layer, rho_layer = gathered(x)
        product = rounded[OWN, 0, x] * to_bfloat16(advanced(FOREIGN, NS - 1, x))
        phi[x] = phi_layer + weights[0] * product
        rho[x + 1] = rho_layer + charged[0] * product

    loop(2, layers - 2, whole)

    second_half(OWN, 1, own_copies)
    for d in (0, 1):
        edge_pair(d, functools.partial(advance, OWN, 3))

    inner = pl.ds(PAD, half)

    def add(x, carry):
        return carry + phi[x, inner]

    partial = lax.fori_loop(3, layers - 2, add, phi[2, inner])

    for copy in edges[2:]:
        copy.wait_recv()
    for d in (0, 1):
        psi_v[in_layer(d, 1) + 2] = read_code(edge_in[d, 4], *psi_span)
    for k in (-1, 0):
        make_base(k)
        make_base(layers - 1 - k)

    second_half(FOREIGN, 2, foreign_copies)
    rho_copies = []
    for d in (0, 1):
        edge_pair(d, whole)
        rho_copies.append(pltpu.make_async_remote_copy(
            rho.at[out_layer(d, 0) + 1, inner], rho.at[0 if d else layers + 1, inner],
            rho_send.at[d], rho_recv.at[d], device_id=targets[d], device_id_type=MESH,
        ))
    for x in (0, 1, layers - 2, layers - 1):
        partial = partial + phi[x, inner]
    sums[0] = jnp.sum(
        sum(partial[:, k:k + 128] for k in range(0, partial.shape[1], 128)), axis=0, keepdims=True
    )

    def share(step, carry):
        pltpu.make_async_remote_copy(
            sums.at[0], sums.at[step], sum_send, sum_recv,
            device_id=device(step), device_id_type=MESH,
        ).start()
        return carry

    lax.fori_loop(1, devices, share, 0)
    for copy in rho_copies:
        send(copy)

    others = sums.at[pl.ds(1, devices - 1)]
    pltpu.make_async_copy(others, others, sum_recv).wait()
    cells = float(devices * layers * half * w_hbm.shape[2])
    inverse = cells / jnp.sum(sums[...])
    scaled = inverse * (1.0 / (6.0 + screening))

    def relax_once(x):
        relaxed[x + 1] = base[x + 1] + rho[x + 1] * scaled

    def first(x):
        density_ref[x] = phi[x, inner] * inverse
        relax_once(x)

    loop(0, layers, first)

    def second(x):
        center = relaxed[x + 1]
        total = relaxed[x] + relaxed[x + 2] + around(center, 0) + around(center, 1)
        value = (total - ion_charge(center) + screening * center) * (1.0 / (6.0 + screening))
        potential_ref[x] = (value + rho[x + 1] * scaled)[PAD:PAD + half]

    loop(1, layers - 1, second)
    for copy in rho_copies:
        copy.wait_recv()
    relax_once(-1)
    relax_once(layers)
    outer(second)

    for copy in sent:
        copy.wait_send()
    pltpu.make_async_copy(others, others, sum_send).wait()


def ion_charge(value):
    return (2.0 * screening) * jnp.tanh(0.5 * value)


def body(ends, slabs, w_field, psi_init, start_field, charges):
    layers, rows, depth = w_field.shape
    half = rows // ends
    wide = half + 2 * PAD
    devices = ends * slabs
    stages = slabs.bit_length()
    out = jax.ShapeDtypeStruct((layers, half, depth), jnp.float32)
    dma = pltpu.SemaphoreType.DMA

    def tile(*lead):
        return pltpu.VMEM((*lead, wide, depth), jnp.float32)

    def code(*lead):
        return pltpu.VMEM((*lead, wide, depth), jnp.int16)

    hbm = pl.BlockSpec(memory_space=pltpu.HBM)
    vmem = pl.BlockSpec(memory_space=pltpu.VMEM)
    return pl.pallas_call(
        functools.partial(kernel, ends, slabs),
        out_shape=(out, out),
        in_specs=[hbm, hbm, hbm, hbm],
        out_specs=(vmem, vmem),
        scratch_shapes=[
            pltpu.SMEM((NS + 1,), jnp.int32), tile(layers + 2), tile(layers + 4), tile(layers), tile(layers),
            tile(NS, layers + 2), tile(2, NS, layers + 4), tile(2, NS + 1, layers),
            tile(layers), tile(layers + 2), tile(layers + 2), tile(layers + 2),
            pltpu.VMEM((devices, 1, 128), jnp.float32),
            code(layers), code(layers), code(2, 5), code(2, 5), code(3, 2, 2), code(3, 2, 2),
            pltpu.SemaphoreType.REGULAR((stages,)), dma(()), dma((4, 3)), dma((layers,)), dma((layers,)),
            dma((2, 2)), dma((2, 2)), dma((3, 2, 2)), dma((3, 2, 2)), dma((2,)), dma((2,)), dma(()), dma(()),
        ],
        compiler_params=pltpu.CompilerParams(
            collective_id=0, has_side_effects=True, vmem_limit_bytes=40 * 1024 * 1024
        ),
        name="scf_step",
    )(*[pltpu.with_memory_space_constraint(v, pltpu.HBM) for v in (charges, w_field, psi_init, start_field)])


def solution(mesh):
    in_specs = (P("slab", None, None), P("slab", None, None), P("end", "slab", None, None), P())
    out_specs = (P("slab", "end", None), P("slab", "end", None))
    step = functools.partial(body, mesh.shape["end"], mesh.shape["slab"])
    return jax.shard_map(step, mesh=mesh, in_specs=in_specs, out_specs=out_specs, check_vma=False)
```

time: 38.3 us -> 33.4 us (0.87)
  Pallas kernels: 35.9 us -> 31 us
    pallas_call x1, Pallas kernels: 35.9 us -> 31 us  [body(): pl.pallas_call(functools.partial(kernel, ends, slabs), out_shape=(out, ou...]
where the time goes in v2:
time: 33.4 us; the launch traced here: 33.3 us
  Pallas kernels  31 us (93%)
  local copies, waits for them, and re-layouts  1.59 us (5%)
  between operations  0.64 us (2%)
    pallas_call x1, Pallas kernels, body(): pl.pallas_call(functools.partial(kernel, ends, slabs), out_shape=(out, ou...  31 us
    unnamed x2, local copies, waits for them, and re-layouts  1.59 us

profile of v2, /device:TPU:0, one launch (start us, length us, event | category | flops | bytes accessed | tf_op | source)
XLA Modules:
  0.0 33.3 jit_solution(6830960803837913103)
XLA Ops:
  0.6 31.0 %scf_step.1 = (f32[8,64,256]{2,1,0:T(8,128)S(1)}, f32[8,64,256]{2,1,0:T(8,128)S(1)}) custom-call(s32[5]{0:T(128)} %charges_hbm.1, f32[8,128,256]{2,1,0:T(8,128)} %w_hbm.1, f32[8,128,256]{2,1,0:T(8,128)} %psi_hbm.1, f32[1,8,128,256]{3,2,1,0:T(8,128)} %start_hbm.1), custom_call_target="tpu_custom_call" | custom-call | tf_op jit(solution)/shard_map/scf_step/pallas_call | solution.py:430
  31.7 0.8 %copy.8 = f32[8,64,256]{2,1,0:T(8,128)} copy(f32[8,64,256]{2,1,0:T(8,128)S(1)} %get-tuple-element.4) | data formatting | bytes 1048576
  32.5 0.8 %copy.9 = f32[8,64,256]{2,1,0:T(8,128)} copy(f32[8,64,256]{2,1,0:T(8,128)S(1)} %get-tuple-element.5) | data formatting | bytes 1048576

commit v3 on v2

--- a/solution.py
+++ b/solution.py
@@ -10,6 +10,8 @@
 
 NS = 4
 PAD = 8
+EDGE = 4
+LANES = 128
 mobility = 0.15
 screening = 1.0
 OWN, FOREIGN = 0, 1
@@ -32,6 +34,7 @@
     partner = (other, slab)
     layers, rows = w_hbm.shape[0], w_hbm.shape[1]
     half = rows // ends
+    parts = w_hbm.shape[2] // LANES
     devices = ends * slabs
     flat = side * slabs + slab
     delta = 1.0 / NS
@@ -63,17 +66,17 @@
 
     mine, theirs = pieces(side), pieces(other)
     local = []
-    for k, (source, target, first, parts) in enumerate((
+    for k, (source, target, first, pieces_of) in enumerate((
         (start_hbm.at[0], theirs_v, 0, theirs), (w_hbm, w_v, 1, mine),
         (psi_hbm, psi_v, 2, mine), (start_hbm.at[0], start_v, 0, mine),
     )):
         local.append([
             pltpu.make_async_copy(
-                source.at[:, pl.ds(begin, count)],
-                target.at[pl.ds(first, layers), pl.ds(at, count)],
-                local_sem.at[k, n],
+                source.at[:, pl.ds(begin, count), pl.ds(h * LANES, LANES)],
+                target.at[pl.ds(first, layers), h, pl.ds(at, count)],
+                local_sem.at[k, n, h],
             )
-            for n, (begin, at, count) in enumerate(parts)
+            for n, (begin, at, count) in enumerate(pieces_of) for h in range(parts)
         ])
     for copies in local:
         for copy in copies:
@@ -84,11 +87,12 @@
             step(x)
             return carry
 
-        lax.fori_loop(low, high, body, 0)
+        lax.fori_loop(low, high, body, 0, unroll=True)
 
     def span(t):
         reach = 0.5 * delta * (W_MAX + PSI_MAX) * t + MARGIN
-        return math.log(START_MIN) - reach, math.log(START_MAX) + reach
+        shift = 0.5 * math.log(mobility) if t else 0.0
+        return math.log(START_MIN) - reach + shift, math.log(START_MAX) + reach + shift
 
     def write_code(value, low, high):
         scaled = value * (CODES / (high - low)) + (0.5 - low * (CODES / (high - low)))
@@ -119,9 +123,11 @@
     pair = [0.5 * (q[k] + q[k + 1]) for k in range(NS)]
 
     def make_factor(x):
-        w, psi = w_v[x + 1], psi_v[x + 2]
-        for k in range(NS):
-            factor[k, x + 1] = jnp.exp(-0.5 * delta * (w + pair[k] * psi))
+        for h in range(parts):
+            level = 0.5 * math.log(mobility) - 0.5 * delta * w_v[x + 1, h]
+            psi = psi_v[x + 2, h]
+            for k in range(NS):
+                factor[k, x + 1, h] = jnp.exp(level - (0.5 * delta * pair[k]) * psi)
 
     def index(chain, t):
         return t if chain == OWN else NS - 1 - t
@@ -129,27 +135,47 @@
     def to_bfloat16(value):
         return value.astype(jnp.bfloat16).astype(jnp.float32)
 
+    window = pl.ds(EDGE, half + 2 * (PAD - EDGE))
+    inner = pl.ds(PAD - EDGE, half)
+
     def begin_chain(chain, x):
         value = start_v[x] if chain == OWN else read_log(field_in[x], 0)
+        u[chain, 0, x + 2] = factor[index(chain, 0), x + 1] * value
         rounded[chain, 0, x] = to_bfloat16(value)
-        u[chain, 0, x + 2] = factor[index(chain, 0), x + 1] * value
-
-    def around(value, axis):
-        return pltpu.roll(value, 1, axis) + pltpu.roll(value, value.shape[axis] - 1, axis)
+
+    lane = lax.broadcasted_iota(jnp.int32, (1, LANES), 1)
+    lowest, highest = lane == 0, lane == LANES - 1
+
+    def around(ref, at, first, count):
+        center = [ref[(*at, h, pl.ds(first, count))] for h in range(parts)]
+        lower = [pltpu.roll(value, 1, 1) for value in center]
+        upper = [pltpu.roll(value, LANES - 1, 1) for value in center]
+        sums = []
+        for h in range(parts):
+            total = ref[(*at, h, pl.ds(first - 1, count))] + ref[(*at, h, pl.ds(first + 1, count))]
+            total = total + jnp.where(lowest, lower[h - 1], lower[h])
+            sums.append(total + jnp.where(highest, upper[(h + 1) % parts], upper[h]))
+        return center, sums
 
     def advanced(chain, t, x):
-        center = u[chain, t, x + 2]
-        total = u[chain, t, x + 1] + u[chain, t, x + 3] + around(center, 0) + around(center, 1)
-        return factor[index(chain, t), x + 1] * ((1.0 - 6.0 * mobility) * center + mobility * total)
+        center, sums = around(u, (chain, t, x + 2), EDGE, window.size)
+        return [
+            factor[index(chain, t), x + 1, h, window] * (
+                (u[chain, t, x + 1, h, window] + u[chain, t, x + 3, h, window])
+                + (sums[h] + ((1.0 - 6.0 * mobility) / mobility) * center[h])
+            )
+            for h in range(parts)
+        ]
 
     def advance_halo(chain, t, x):
-        u[chain, t + 1, x + 2] = factor[index(chain, t + 1), x + 1] * advanced(chain, t, x)
+        for h, value in enumerate(advanced(chain, t, x)):
+            u[chain, t + 1, x + 2, h, window] = factor[index(chain, t + 1), x + 1, h, window] * value
 
     def advance(chain, t, x):
-        value = advanced(chain, t, x)
-        rounded[chain, t + 1, x] = to_bfloat16(value)
-        if t + 1 < NS:
-            u[chain, t + 1, x + 2] = factor[index(chain, t + 1), x + 1] * value
+        for h, value in enumerate(advanced(chain, t, x)):
+            rounded[chain, t + 1, x, h, window] = to_bfloat16(value)
+            if t + 1 < NS:
+                u[chain, t + 1, x + 2, h, window] = factor[index(chain, t + 1), x + 1, h, window] * value
 
     def adv(chain, t, low, high):
         loop(low, high, functools.partial(advance, chain, t))
@@ -186,11 +212,18 @@
         edge_out[d, 2] = write_code(w_v[out_layer(d, 0) + 1], *w_span)
     adv(OWN, 0, 1, layers - 1)
     adv(OWN, 1, 2, layers - 2)
+    adv(OWN, 2, 3, layers - 3)
+
+    def relaxation(center, total):
+        return (total - ion_charge(center) + screening * center) * (1.0 / (6.0 + screening))
 
     def make_base(x):
-        center = psi_v[x + 2]
-        total = psi_v[x + 1] + psi_v[x + 3] + around(center, 0) + around(center, 1)
-        base[x + 1] = (total - ion_charge(center) + screening * center) * (1.0 / (6.0 + screening))
+        center, sums = around(psi_v, (x + 2,), EDGE, window.size)
+        for h in range(parts):
+            total = psi_v[x + 1, h, window] + psi_v[x + 3, h, window] + sums[h]
+            base[x + 1, h] = relaxation(center[h], total)
+
+    loop(1, layers - 1, make_base)
 
     groups = [(0, layers - 1), (1, layers - 2), (2, layers - 3), tuple(range(3, layers - 3))]
     order = [x for group in groups for x in group]
@@ -235,9 +268,7 @@
             open_gate(stage + 1)
 
     open_gate(0)
-    adv(OWN, 2, 3, layers - 3)
     pass_gate(0)
-    loop(1, layers - 1, make_base)
     pass_gate(1)
 
     def arrive(group):
@@ -254,10 +285,6 @@
             copies.append(send(halo(0, d, j, 1)))
 
     pass_gate(2)
-    arrive(2)
-    adv(FOREIGN, 0, 1, 2)
-    adv(FOREIGN, 0, layers - 2, layers - 1)
-
     for copy in edges[:2]:
         copy.wait_recv()
     for d in (0, 1):
@@ -280,11 +307,18 @@
         return result
 
     own_copies = half_way(OWN, 1)
+    adv(OWN, 2, 1, 3)
+    adv(OWN, 2, layers - 3, layers - 1)
+    adv(OWN, 3, 2, layers - 2)
 
     pass_gate(3)
+    arrive(2)
+    adv(FOREIGN, 0, 1, 2)
+    adv(FOREIGN, 0, layers - 2, layers - 1)
     arrive(3)
     adv(FOREIGN, 0, 2, layers - 2)
     adv(FOREIGN, 1, 2, layers - 2)
+    adv(FOREIGN, 2, 3, layers - 3)
     for copy in copies:
         copy.wait_recv()
     for d in (0, 1):
@@ -296,10 +330,8 @@
 
     for stage in range(4, stages):
         pass_gate(stage)
-    adv(OWN, 2, 1, 3)
-    adv(OWN, 2, layers - 3, layers - 1)
-    adv(OWN, 3, 2, layers - 2)
-    adv(FOREIGN, 2, 1, layers - 1)
+    adv(FOREIGN, 2, 1, 3)
+    adv(FOREIGN, 2, layers - 3, layers - 1)
 
     def second_half(chain, kind, copies):
         for copy in copies:
@@ -310,22 +342,35 @@
         beyond(functools.partial(advance_halo, chain, 2))
         outer(functools.partial(advance, chain, 2))
 
-    weights = [delta * (0.5 if t in (0, NS) else 1.0) for t in range(NS + 1)]
+    weights = [0.5 if t in (0, NS) else 1.0 for t in range(NS + 1)]
     charged = [weights[t] * q[t] for t in range(NS + 1)]
 
-    def gathered(x):
+    def gathered(x, h, terms):
         phi_layer, rho_layer = 0.0, 0.0
-        for t in range(1, NS + 1):
-            product = rounded[OWN, t, x] * rounded[FOREIGN, NS - t, x]
-            phi_layer = phi_layer + weights[t] * product
+        for t in terms:
+            product = rounded[OWN, t, x, h, window] * rounded[FOREIGN, NS - t, x, h, window]
+            phi_layer = phi_layer + (product if weights[t] == 1.0 else weights[t] * product)
             rho_layer = rho_layer + charged[t] * product
         return phi_layer, rho_layer
 
+    def gather(x):
+        for h in range(parts):
+            phi[x, h], rho[x + 1, h] = gathered(x, h, range(2, NS + 1))
+
+    def complete(x, early):
+        for h, value in enumerate(advanced(FOREIGN, NS - 1, x)):
+            phi_layer, rho_layer = gathered(x, h, range(1, 2 if early else NS + 1))
+            product = rounded[OWN, 0, x, h, window] * to_bfloat16(value)
+            phi_layer = phi_layer + weights[0] * product
+            rho_layer = rho_layer + charged[0] * product
+            phi[x, h] = phi[x, h] + phi_layer if early else phi_layer
+            rho[x + 1, h] = rho[x + 1, h] + rho_layer if early else rho_layer
+
     def whole(x):
-        phi_layer, rho_layer = gathered(x)
-        product = rounded[OWN, 0, x] * to_bfloat16(advanced(FOREIGN, NS - 1, x))
-        phi[x] = phi_layer + weights[0] * product
-        rho[x + 1] = rho_layer + charged[0] * product
+        complete(x, False)
+
+    def finish(x):
+        complete(x, True)
 
     loop(2, layers - 2, whole)
 
@@ -333,12 +378,13 @@
     for d in (0, 1):
         edge_pair(d, functools.partial(advance, OWN, 3))
 
-    inner = pl.ds(PAD, half)
-
-    def add(x, carry):
-        return carry + phi[x, inner]
-
-    partial = lax.fori_loop(3, layers - 2, add, phi[2, inner])
+    def cells_of(x):
+        return sum(phi[x, h, inner] for h in range(parts))
+
+    partial = sum(cells_of(x) for x in range(2, layers - 2))
+
+    for d in (0, 1):
+        edge_pair(d, gather)
 
     for copy in edges[2:]:
         copy.wait_recv()
@@ -351,16 +397,14 @@
     second_half(FOREIGN, 2, foreign_copies)
     rho_copies = []
     for d in (0, 1):
-        edge_pair(d, whole)
+        edge_pair(d, finish)
         rho_copies.append(pltpu.make_async_remote_copy(
-            rho.at[out_layer(d, 0) + 1, inner], rho.at[0 if d else layers + 1, inner],
+            rho.at[out_layer(d, 0) + 1], rho.at[0 if d else layers + 1],
             rho_send.at[d], rho_recv.at[d], device_id=targets[d], device_id_type=MESH,
         ))
     for x in (0, 1, layers - 2, layers - 1):
-        partial = partial + phi[x, inner]
-    sums[0] = jnp.sum(
-        sum(partial[:, k:k + 128] for k in range(0, partial.shape[1], 128)), axis=0, keepdims=True
-    )
+        partial = partial + cells_of(x)
+    sums[0] = jnp.sum(partial, axis=0, keepdims=True)
 
     def share(step, carry):
         pltpu.make_async_remote_copy(
@@ -380,19 +424,22 @@
     scaled = inverse * (1.0 / (6.0 + screening))
 
     def relax_once(x):
-        relaxed[x + 1] = base[x + 1] + rho[x + 1] * scaled
+        for h in range(parts):
+            relaxed[x + 1, h] = base[x + 1, h] + rho[x + 1, h] * scaled
 
     def first(x):
-        density_ref[x] = phi[x, inner] * inverse
+        for h in range(parts):
+            density_ref[x, :, h * LANES:(h + 1) * LANES] = phi[x, h, inner] * inverse
         relax_once(x)
 
     loop(0, layers, first)
 
     def second(x):
-        center = relaxed[x + 1]
-        total = relaxed[x] + relaxed[x + 2] + around(center, 0) + around(center, 1)
-        value = (total - ion_charge(center) + screening * center) * (1.0 / (6.0 + screening))
-        potential_ref[x] = (value + rho[x + 1] * scaled)[PAD:PAD + half]
+        center, sums = around(relaxed, (x + 1,), PAD - EDGE, half)
+        for h in range(parts):
+            total = relaxed[x, h, inner] + relaxed[x + 2, h, inner] + sums[h]
+            value = relaxation(center[h], total) + rho[x + 1, h, inner] * scaled
+            potential_ref[x, :, h * LANES:(h + 1) * LANES] = value
 
     loop(1, layers - 1, second)
     for copy in rho_copies:
@@ -419,11 +466,17 @@
     out = jax.ShapeDtypeStruct((layers, half, depth), jnp.float32)
     dma = pltpu.SemaphoreType.DMA
 
+    parts = depth // LANES
+    narrow = half + 2 * (PAD - EDGE)
+
     def tile(*lead):
-        return pltpu.VMEM((*lead, wide, depth), jnp.float32)
+        return pltpu.VMEM((*lead, parts, wide, LANES), jnp.float32)
+
+    def slim(*lead):
+        return pltpu.VMEM((*lead, parts, narrow, LANES), jnp.float32)
 
     def code(*lead):
-        return pltpu.VMEM((*lead, wide, depth), jnp.int16)
+        return pltpu.VMEM((*lead, parts, wide, LANES), jnp.int16)
 
     hbm = pl.BlockSpec(memory_space=pltpu.HBM)
     vmem = pl.BlockSpec(memory_space=pltpu.VMEM)
@@ -435,10 +488,10 @@
         scratch_shapes=[
             pltpu.SMEM((NS + 1,), jnp.int32), tile(layers + 2), tile(layers + 4), tile(layers), tile(layers),
             tile(NS, layers + 2), tile(2, NS, layers + 4), tile(2, NS + 1, layers),
-            tile(layers), tile(layers + 2), tile(layers + 2), tile(layers + 2),
+            slim(layers), slim(layers + 2), slim(layers + 2), slim(layers + 2),
             pltpu.VMEM((devices, 1, 128), jnp.float32),
             code(layers), code(layers), code(2, 5), code(2, 5), code(3, 2, 2), code(3, 2, 2),
-            pltpu.SemaphoreType.REGULAR((stages,)), dma(()), dma((4, 3)), dma((layers,)), dma((layers,)),
+            pltpu.SemaphoreType.REGULAR((stages,)), dma(()), dma((4, 3, parts)), dma((layers,)), dma((layers,)),
             dma((2, 2)), dma((2, 2)), dma((3, 2, 2)), dma((3, 2, 2)), dma((2,)), dma((2,)), dma(()), dma(()),
         ],
         compiler_params=pltpu.CompilerParams(

time: 33.4 us -> 29.4 us (0.88)
  Pallas kernels: 31 us -> 27 us
    pallas_call x1, Pallas kernels: 31 us -> 27 us  [body(): pl.pallas_call(functools.partial(kernel, ends, slabs), out_shape=(out, ou...]
where the time goes in v3:
time: 29.4 us; the launch traced here: 29.2 us
  Pallas kernels  27 us (92%)
  local copies, waits for them, and re-layouts  1.59 us (5%)
  between operations  0.64 us (2%)
    pallas_call x1, Pallas kernels, body(): pl.pallas_call(functools.partial(kernel, ends, slabs), out_shape=(out, ou...  27 us
    unnamed x2, local copies, waits for them, and re-layouts  1.59 us

profile of v3, /device:TPU:0, one launch (start us, length us, event | category | flops | bytes accessed | tf_op | source)
XLA Modules:
  0.0 29.2 jit_solution(9673807546105111567)
XLA Ops:
  0.6 27.0 %scf_step.1 = (f32[8,64,256]{2,1,0:T(8,128)S(1)}, f32[8,64,256]{2,1,0:T(8,128)S(1)}) custom-call(s32[5]{0:T(128)} %charges_hbm.1, f32[8,128,256]{2,1,0:T(8,128)} %w_hbm.1, f32[8,128,256]{2,1,0:T(8,128)} %psi_hbm.1, f32[1,8,128,256]{3,2,1,0:T(8,128)} %start_hbm.1), custom_call_target="tpu_custom_call" | custom-call | tf_op jit(solution)/shard_map/scf_step/pallas_call | solution.py:483
  27.7 0.8 %copy.8 = f32[8,64,256]{2,1,0:T(8,128)} copy(f32[8,64,256]{2,1,0:T(8,128)S(1)} %get-tuple-element.4) | data formatting | bytes 1048576
  28.5 0.8 %copy.9 = f32[8,64,256]{2,1,0:T(8,128)} copy(f32[8,64,256]{2,1,0:T(8,128)S(1)} %get-tuple-element.5) | data formatting | bytes 1048576

commit v4 on v3

--- a/solution.py
+++ b/solution.py
@@ -24,8 +24,8 @@
 
 def kernel(ends, slabs, charges_hbm, w_hbm, psi_hbm, start_hbm, density_ref, potential_ref,
            charges_ref, w_v, psi_v, start_v, theirs_v, factor, u, rounded, phi, rho, base, relaxed, sums,
-           field_out, field_in, edge_out, edge_in, halo_out, halo_in,
-           gate, charges_sem, local_sem, field_send, field_recv, edge_send, edge_recv, halo_send, halo_recv,
+           field_out, field_in, edge_out, edge_in, halo_out, halo_in, rho_out, rho_in,
+           gate, charges_sem, field_sem, local_sem, field_send, field_recv, edge_send, edge_recv, halo_send, halo_recv,
            rho_send, rho_recv, sum_send, sum_recv):
     side, slab = lax.axis_index("end"), lax.axis_index("slab")
     other = lax.rem(side + 1, ends)
@@ -53,8 +53,16 @@
         near.append((side, slab + width - 2 * width * lax.rem(slab // width, 2)))
         width *= 2
     near.append(partner)
-    for neighbour in near + [left, right]:
+    for neighbour in near:
         pl.semaphore_signal(barrier, inc=1, device_id=neighbour, device_id_type=MESH)
+    targets = (left, right)
+    seams = (slab == 0, slab == slabs - 1)
+    for d in (0, 1):
+        @pl.when(jnp.logical_not(seams[d]))
+        def _(d=d):
+            pl.semaphore_signal(barrier, inc=1, device_id=targets[d], device_id_type=MESH)
+
+    greeted = len(near) + jnp.where(slab % (slabs - 1) == 0, 1, 2)
 
     def pieces(which):
         first = which * half
@@ -65,22 +73,36 @@
         )
 
     mine, theirs = pieces(side), pieces(other)
-    local = []
-    for k, (source, target, first, pieces_of) in enumerate((
-        (start_hbm.at[0], theirs_v, 0, theirs), (w_hbm, w_v, 1, mine),
-        (psi_hbm, psi_v, 2, mine), (start_hbm.at[0], start_v, 0, mine),
-    )):
-        local.append([
+    groups = [(0, layers - 1), (1, layers - 2), (2, layers - 3), tuple(range(3, layers - 3))]
+    order = [x for group in groups for x in group]
+    field_copies = {
+        x: [
             pltpu.make_async_copy(
-                source.at[:, pl.ds(begin, count), pl.ds(h * LANES, LANES)],
-                target.at[pl.ds(first, layers), h, pl.ds(at, count)],
-                local_sem.at[k, n, h],
+                start_hbm.at[0, x, pl.ds(begin, count)], theirs_v.at[x, pl.ds(at, count)], field_sem.at[x, n],
             )
-            for n, (begin, at, count) in enumerate(pieces_of) for h in range(parts)
-        ])
-    for copies in local:
-        for copy in copies:
+            for n, (begin, at, count) in enumerate(theirs)
+        ]
+        for x in order
+    }
+    for x in order:
+        for copy in field_copies[x]:
             copy.start()
+    local = [
+        pltpu.make_async_copy(
+            source.at[:, pl.ds(begin, count)], target.at[pl.ds(first, layers), pl.ds(at, count)], local_sem.at[k, n],
+        )
+        for k, (source, target, first) in enumerate(((w_hbm, w_v, 1), (start_hbm.at[0], start_v, 0)))
+        for n, (begin, at, count) in enumerate(mine)
+    ]
+    local += [
+        pltpu.make_async_copy(
+            psi_hbm.at[:, pl.ds(begin, count), pl.ds(h * LANES, LANES)],
+            psi_v.at[pl.ds(2, layers), h, pl.ds(at, count)], local_sem.at[2 + h, n],
+        )
+        for n, (begin, at, count) in enumerate(mine) for h in range(parts)
+    ]
+    for copy in local:
+        copy.start()
 
     def loop(low, high, step):
         def body(x, carry):
@@ -110,13 +132,30 @@
 
     w_span, psi_span = (-W_MAX - MARGIN, W_MAX + MARGIN), (-PSI_MAX - MARGIN, PSI_MAX + MARGIN)
 
-    for copy in local[0]:
-        copy.wait()
-
-    def code_field(x):
-        field_out[x] = write_log(theirs_v[x], 0)
-
-    loop(0, layers, code_field)
+    sent = []
+
+    def send(copy):
+        copy.start()
+        sent.append(copy)
+        return copy
+
+    def plane(h):
+        return slice(h * LANES, (h + 1) * LANES)
+
+    fields = {}
+    for group in groups:
+        for x in group:
+            for copy in field_copies[x]:
+                copy.wait()
+            for h in range(parts):
+                field_out[x, h] = write_log(theirs_v[x, :, plane(h)], 0)
+        if not fields:
+            pl.semaphore_wait(barrier, greeted)
+        for x in group:
+            fields[x] = send(pltpu.make_async_remote_copy(
+                field_out.at[x], field_in.at[x], field_send.at[x], field_recv.at[x],
+                device_id=partner, device_id_type=MESH,
+            ))
 
     charges_copy.wait()
     q = [charges_ref[side * (NS - 2 * t) + t].astype(jnp.float32) for t in range(NS + 1)]
@@ -124,7 +163,7 @@
 
     def make_factor(x):
         for h in range(parts):
-            level = 0.5 * math.log(mobility) - 0.5 * delta * w_v[x + 1, h]
+            level = 0.5 * math.log(mobility) - 0.5 * delta * w_v[x + 1, :, plane(h)]
             psi = psi_v[x + 2, h]
             for k in range(NS):
                 factor[k, x + 1, h] = jnp.exp(level - (0.5 * delta * pair[k]) * psi)
@@ -139,9 +178,10 @@
     inner = pl.ds(PAD - EDGE, half)
 
     def begin_chain(chain, x):
-        value = start_v[x] if chain == OWN else read_log(field_in[x], 0)
-        u[chain, 0, x + 2] = factor[index(chain, 0), x + 1] * value
-        rounded[chain, 0, x] = to_bfloat16(value)
+        for h in range(parts):
+            value = start_v[x, :, plane(h)] if chain == OWN else read_log(field_in[x, h], 0)
+            u[chain, 0, x + 2, h] = factor[index(chain, 0), x + 1, h] * value
+            rounded[chain, 0, x, h] = to_bfloat16(value)
 
     lane = lax.broadcasted_iota(jnp.int32, (1, LANES), 1)
     lowest, highest = lane == 0, lane == LANES - 1
@@ -195,23 +235,54 @@
     def in_layer(d, j):
         return -1 - j if d else layers + j
 
-    targets = (left, right)
-
-    for copies in local[1:]:
-        for copy in copies:
-            copy.wait()
-    loop(0, layers, make_factor)
-    loop(0, layers, functools.partial(begin_chain, OWN))
-    for d in (0, 1):
+    for copy in local:
+        copy.wait()
+    for d in (0, 1):
+        edge_pair(d, make_factor)
+        edge_pair(d, functools.partial(begin_chain, OWN))
+
         def code_edge(j, d=d):
             x = out_layer(d, j)
             edge_out[d, j] = write_log(u[OWN, 0, x + 2], 1)
             edge_out[d, 3 + j] = write_code(psi_v[x + 2], *psi_span)
 
         loop(0, 2, code_edge)
-        edge_out[d, 2] = write_code(w_v[out_layer(d, 0) + 1], *w_span)
+        for h in range(parts):
+            edge_out[d, 2, h] = write_code(w_v[out_layer(d, 0) + 1, :, plane(h)], *w_span)
+    edges = [
+        pltpu.make_async_remote_copy(
+            edge_out.at[d, pl.ds(first, count)], edge_in.at[d, pl.ds(first, count)],
+            edge_send.at[d, n], edge_recv.at[d, n], device_id=targets[d], device_id_type=MESH,
+        )
+        for n, (first, count) in enumerate(((0, 4), (4, 1))) for d in (0, 1)
+    ]
+    sent += edges
+
+    def send_edges(seam):
+        for d in (0, 1):
+            @pl.when(seams[d] if seam else jnp.logical_not(seams[d]))
+            def _(d=d):
+                edges[d].start()
+                edges[2 + d].start()
+
+    send_edges(False)
+    stages = len(near)
+
+    def open_gate(stage):
+        pl.semaphore_signal(gate.at[stage], inc=1, device_id=near[stage], device_id_type=MESH)
+
+    def pass_gate(stage):
+        pl.semaphore_wait(gate.at[stage], 1)
+        if stage + 1 < stages:
+            open_gate(stage + 1)
+
+    open_gate(0)
+    loop(2, layers - 2, make_factor)
+    loop(2, layers - 2, functools.partial(begin_chain, OWN))
+    pass_gate(0)
     adv(OWN, 0, 1, layers - 1)
     adv(OWN, 1, 2, layers - 2)
+    pass_gate(1)
     adv(OWN, 2, 3, layers - 3)
 
     def relaxation(center, total):
@@ -224,31 +295,9 @@
             base[x + 1, h] = relaxation(center[h], total)
 
     loop(1, layers - 1, make_base)
-
-    groups = [(0, layers - 1), (1, layers - 2), (2, layers - 3), tuple(range(3, layers - 3))]
-    order = [x for group in groups for x in group]
-    sent = []
-
-    def send(copy):
-        copy.start()
-        sent.append(copy)
-        return copy
-
-    pl.semaphore_wait(barrier, len(near) + 2)
-    fields = {
-        x: send(pltpu.make_async_remote_copy(
-            field_out.at[x], field_in.at[x], field_send.at[x], field_recv.at[x],
-            device_id=partner, device_id_type=MESH,
-        ))
-        for x in order
-    }
-    edges = [
-        send(pltpu.make_async_remote_copy(
-            edge_out.at[d, pl.ds(first, count)], edge_in.at[d, pl.ds(first, count)],
-            edge_send.at[d, n], edge_recv.at[d, n], device_id=targets[d], device_id_type=MESH,
-        ))
-        for n, (first, count) in enumerate(((0, 4), (4, 1))) for d in (0, 1)
-    ]
+    for stage in range(2, stages - 1):
+        pass_gate(stage)
+    send_edges(True)
 
     def halo(kind, d, first, count):
         return pltpu.make_async_remote_copy(
@@ -257,20 +306,6 @@
             device_id=targets[d], device_id_type=MESH,
         )
 
-    stages = len(near)
-
-    def open_gate(stage):
-        pl.semaphore_signal(gate.at[stage], inc=1, device_id=near[stage], device_id_type=MESH)
-
-    def pass_gate(stage):
-        pl.semaphore_wait(gate.at[stage], 1)
-        if stage + 1 < stages:
-            open_gate(stage + 1)
-
-    open_gate(0)
-    pass_gate(0)
-    pass_gate(1)
-
     def arrive(group):
         for x in groups[group]:
             fields[x].wait_recv()
@@ -284,12 +319,12 @@
             halo_out[0, d, j] = write_log(u[FOREIGN, 0, out_layer(d, j) + 2], 1)
             copies.append(send(halo(0, d, j, 1)))
 
-    pass_gate(2)
     for copy in edges[:2]:
         copy.wait_recv()
     for d in (0, 1):
         x = in_layer(d, 0)
-        w_v[x + 1] = read_code(edge_in[d, 2], *w_span)
+        for h in range(parts):
+            w_v[x + 1, :, plane(h)] = read_code(edge_in[d, 2, h], *w_span)
         psi_v[x + 2] = read_code(edge_in[d, 3], *psi_span)
         for j in (0, 1):
             u[OWN, 0, in_layer(d, j) + 2] = read_log(edge_in[d, j], 1)
@@ -311,7 +346,6 @@
     adv(OWN, 2, layers - 3, layers - 1)
     adv(OWN, 3, 2, layers - 2)
 
-    pass_gate(3)
     arrive(2)
     adv(FOREIGN, 0, 1, 2)
     adv(FOREIGN, 0, layers - 2, layers - 1)
@@ -328,8 +362,7 @@
     outer(functools.partial(advance, FOREIGN, 0))
     foreign_copies = half_way(FOREIGN, 2)
 
-    for stage in range(4, stages):
-        pass_gate(stage)
+    pass_gate(stages - 1)
     adv(FOREIGN, 2, 1, 3)
     adv(FOREIGN, 2, layers - 3, layers - 1)
 
@@ -398,10 +431,10 @@
     rho_copies = []
     for d in (0, 1):
         edge_pair(d, finish)
-        rho_copies.append(pltpu.make_async_remote_copy(
-            rho.at[out_layer(d, 0) + 1], rho.at[0 if d else layers + 1],
-            rho_send.at[d], rho_recv.at[d], device_id=targets[d], device_id_type=MESH,
-        ))
+        rho_out[d] = rho[out_layer(d, 0) + 1].astype(jnp.bfloat16)
+        rho_copies.append(send(pltpu.make_async_remote_copy(
+            rho_out.at[d], rho_in.at[d], rho_send.at[d], rho_recv.at[d], device_id=targets[d], device_id_type=MESH,
+        )))
     for x in (0, 1, layers - 2, layers - 1):
         partial = partial + cells_of(x)
     sums[0] = jnp.sum(partial, axis=0, keepdims=True)
@@ -414,8 +447,6 @@
         return carry
 
     lax.fori_loop(1, devices, share, 0)
-    for copy in rho_copies:
-        send(copy)
 
     others = sums.at[pl.ds(1, devices - 1)]
     pltpu.make_async_copy(others, others, sum_recv).wait()
@@ -444,8 +475,9 @@
     loop(1, layers - 1, second)
     for copy in rho_copies:
         copy.wait_recv()
-    relax_once(-1)
-    relax_once(layers)
+    for d in (0, 1):
+        rho[in_layer(d, 0) + 1] = rho_in[d].astype(jnp.float32)
+        relax_once(in_layer(d, 0))
     outer(second)
 
     for copy in sent:
@@ -475,6 +507,11 @@
     def slim(*lead):
         return pltpu.VMEM((*lead, parts, narrow, LANES), jnp.float32)
 
+    def whole_rows(*lead):
+        return pltpu.VMEM((*lead, wide, depth), jnp.float32)
+
+    edge_rho = pltpu.VMEM((2, parts, narrow, LANES), jnp.bfloat16)
+
     def code(*lead):
         return pltpu.VMEM((*lead, parts, wide, LANES), jnp.int16)
 
@@ -486,12 +523,12 @@
         in_specs=[hbm, hbm, hbm, hbm],
         out_specs=(vmem, vmem),
         scratch_shapes=[
-            pltpu.SMEM((NS + 1,), jnp.int32), tile(layers + 2), tile(layers + 4), tile(layers), tile(layers),
+            pltpu.SMEM((NS + 1,), jnp.int32), whole_rows(layers + 2), tile(layers + 4), whole_rows(layers), whole_rows(layers),
             tile(NS, layers + 2), tile(2, NS, layers + 4), tile(2, NS + 1, layers),
             slim(layers), slim(layers + 2), slim(layers + 2), slim(layers + 2),
-            pltpu.VMEM((devices, 1, 128), jnp.float32),
-            code(layers), code(layers), code(2, 5), code(2, 5), code(3, 2, 2), code(3, 2, 2),
-            pltpu.SemaphoreType.REGULAR((stages,)), dma(()), dma((4, 3, parts)), dma((layers,)), dma((layers,)),
+            pltpu.VMEM((devices, 1, LANES), jnp.float32),
+            code(layers), code(layers), code(2, 5), code(2, 5), code(3, 2, 2), code(3, 2, 2), edge_rho, edge_rho,
+            pltpu.SemaphoreType.REGULAR((stages,)), dma(()), dma((layers, 3)), dma((2 + parts, 3)), dma((layers,)), dma((layers,)),
             dma((2, 2)), dma((2, 2)), dma((3, 2, 2)), dma((3, 2, 2)), dma((2,)), dma((2,)), dma(()), dma(()),
         ],
         compiler_params=pltpu.CompilerParams(

time: 29.4 us -> 30 us (1.020)
  Pallas kernels: 27 us -> 27.6 us
    pallas_call x1, Pallas kernels: 27 us -> 27.6 us  [body(): pl.pallas_call(functools.partial(kernel, ends, slabs), out_shape=(out, ou...]
where the time goes in v4:
time: 30 us; the launch traced here: 29.8 us
  Pallas kernels  27.6 us (92%)
  local copies, waits for them, and re-layouts  1.59 us (5%)
  between operations  0.64 us (2%)
    pallas_call x1, Pallas kernels, body(): pl.pallas_call(functools.partial(kernel, ends, slabs), out_shape=(out, ou...  27.6 us
    unnamed x2, local copies, waits for them, and re-layouts  1.59 us

profile of v4, /device:TPU:0, one launch (start us, length us, event | category | flops | bytes accessed | tf_op | source)
XLA Modules:
  0.0 29.8 jit_solution(7434230725737871945)
XLA Ops:
  0.6 27.6 %scf_step.1 = (f32[8,64,256]{2,1,0:T(8,128)S(1)}, f32[8,64,256]{2,1,0:T(8,128)S(1)}) custom-call(s32[5]{0:T(128)} %charges_hbm.1, f32[8,128,256]{2,1,0:T(8,128)} %w_hbm.1, f32[8,128,256]{2,1,0:T(8,128)} %psi_hbm.1, f32[1,8,128,256]{3,2,1,0:T(8,128)} %start_hbm.1), custom_call_target="tpu_custom_call" | custom-call | tf_op jit(solution)/shard_map/scf_step/pallas_call | solution.py:520
  28.2 0.8 %copy.8 = f32[8,64,256]{2,1,0:T(8,128)} copy(f32[8,64,256]{2,1,0:T(8,128)S(1)} %get-tuple-element.4) | data formatting | bytes 1048576
  29.0 0.8 %copy.9 = f32[8,64,256]{2,1,0:T(8,128)} copy(f32[8,64,256]{2,1,0:T(8,128)S(1)} %get-tuple-element.5) | data formatting | bytes 1048576

commit v5 on v4

--- a/solution.py
+++ b/solution.py
@@ -25,7 +25,7 @@
 def kernel(ends, slabs, charges_hbm, w_hbm, psi_hbm, start_hbm, density_ref, potential_ref,
            charges_ref, w_v, psi_v, start_v, theirs_v, factor, u, rounded, phi, rho, base, relaxed, sums,
            field_out, field_in, edge_out, edge_in, halo_out, halo_in, rho_out, rho_in,
-           gate, charges_sem, field_sem, local_sem, field_send, field_recv, edge_send, edge_recv, halo_send, halo_recv,
+           gate, seam_gate, charges_sem, field_sem, local_sem, field_send, field_recv, edge_send, edge_recv, halo_send, halo_recv,
            rho_send, rho_recv, sum_send, sum_recv):
     side, slab = lax.axis_index("end"), lax.axis_index("slab")
     other = lax.rem(side + 1, ends)
@@ -39,8 +39,8 @@
     flat = side * slabs + slab
     delta = 1.0 / NS
 
-    def device(step):
-        target = lax.rem(flat + step, devices)
+    def device(distance):
+        target = lax.rem(flat + distance, devices)
         return (target // slabs, lax.rem(target, slabs))
 
     barrier = pltpu.get_barrier_semaphore()
@@ -53,16 +53,16 @@
         near.append((side, slab + width - 2 * width * lax.rem(slab // width, 2)))
         width *= 2
     near.append(partner)
-    for neighbour in near:
+    first_slab, last_slab = slab == 0, slab == slabs - 1
+    for neighbour in near + [left]:
         pl.semaphore_signal(barrier, inc=1, device_id=neighbour, device_id_type=MESH)
+
+    @pl.when(jnp.logical_not(last_slab))
+    def _():
+        pl.semaphore_signal(barrier, inc=1, device_id=right, device_id_type=MESH)
+
+    greeted = len(near) + jnp.where(first_slab, 1, 2)
     targets = (left, right)
-    seams = (slab == 0, slab == slabs - 1)
-    for d in (0, 1):
-        @pl.when(jnp.logical_not(seams[d]))
-        def _(d=d):
-            pl.semaphore_signal(barrier, inc=1, device_id=targets[d], device_id_type=MESH)
-
-    greeted = len(near) + jnp.where(slab % (slabs - 1) == 0, 1, 2)
 
     def pieces(which):
         first = which * half
@@ -74,35 +74,30 @@
 
     mine, theirs = pieces(side), pieces(other)
     groups = [(0, layers - 1), (1, layers - 2), (2, layers - 3), tuple(range(3, layers - 3))]
-    order = [x for group in groups for x in group]
-    field_copies = {
-        x: [
+    firsts = [sum(len(group) for group in groups[:k]) for k in range(len(groups))]
+    slots = [pl.ds(first, len(group)) for first, group in zip(firsts, groups)]
+    slot_of = {x: first + k for first, group in zip(firsts, groups) for k, x in enumerate(group)}
+    for k, group in enumerate(groups):
+        for x in group:
+            for begin, at, count in theirs:
+                pltpu.make_async_copy(
+                    start_hbm.at[0, x, pl.ds(begin, count)], theirs_v.at[slot_of[x], pl.ds(at, count)], field_sem.at[k],
+                ).start()
+    for begin, at, count in mine:
+        pltpu.make_async_copy(
+            w_hbm.at[:, pl.ds(begin, count)], w_v.at[pl.ds(1, layers), pl.ds(at, count)], local_sem.at[0],
+        ).start()
+        for h in range(parts):
             pltpu.make_async_copy(
-                start_hbm.at[0, x, pl.ds(begin, count)], theirs_v.at[x, pl.ds(at, count)], field_sem.at[x, n],
-            )
-            for n, (begin, at, count) in enumerate(theirs)
-        ]
-        for x in order
-    }
-    for x in order:
-        for copy in field_copies[x]:
-            copy.start()
-    local = [
+                psi_hbm.at[:, pl.ds(begin, count), pl.ds(h * LANES, LANES)],
+                psi_v.at[pl.ds(2, layers), h, pl.ds(at, count)], local_sem.at[1],
+            ).start()
         pltpu.make_async_copy(
-            source.at[:, pl.ds(begin, count)], target.at[pl.ds(first, layers), pl.ds(at, count)], local_sem.at[k, n],
-        )
-        for k, (source, target, first) in enumerate(((w_hbm, w_v, 1), (start_hbm.at[0], start_v, 0)))
-        for n, (begin, at, count) in enumerate(mine)
-    ]
-    local += [
-        pltpu.make_async_copy(
-            psi_hbm.at[:, pl.ds(begin, count), pl.ds(h * LANES, LANES)],
-            psi_v.at[pl.ds(2, layers), h, pl.ds(at, count)], local_sem.at[2 + h, n],
-        )
-        for n, (begin, at, count) in enumerate(mine) for h in range(parts)
-    ]
-    for copy in local:
-        copy.start()
+            start_hbm.at[0, :, pl.ds(begin, count)], start_v.at[:, pl.ds(at, count)], local_sem.at[2],
+        ).start()
+
+    def taken(ref, semaphore):
+        pltpu.make_async_copy(ref, ref, semaphore).wait()
 
     def loop(low, high, step):
         def body(x, carry):
@@ -132,30 +127,25 @@
 
     w_span, psi_span = (-W_MAX - MARGIN, W_MAX + MARGIN), (-PSI_MAX - MARGIN, PSI_MAX + MARGIN)
 
-    sent = []
-
-    def send(copy):
-        copy.start()
-        sent.append(copy)
-        return copy
-
     def plane(h):
         return slice(h * LANES, (h + 1) * LANES)
 
-    fields = {}
-    for group in groups:
+    for k, group in enumerate(groups):
+        taken(theirs_v.at[slots[k]], field_sem.at[k])
         for x in group:
-            for copy in field_copies[x]:
-                copy.wait()
             for h in range(parts):
-                field_out[x, h] = write_log(theirs_v[x, :, plane(h)], 0)
-        if not fields:
+                field_out[slot_of[x], h] = write_log(theirs_v[slot_of[x], :, plane(h)], 0)
+        if k == 0:
             pl.semaphore_wait(barrier, greeted)
-        for x in group:
-            fields[x] = send(pltpu.make_async_remote_copy(
-                field_out.at[x], field_in.at[x], field_send.at[x], field_recv.at[x],
-                device_id=partner, device_id_type=MESH,
-            ))
+
+            @pl.when(last_slab)
+            def _():
+                pl.semaphore_signal(seam_gate, inc=1, device_id=right, device_id_type=MESH)
+
+        pltpu.make_async_remote_copy(
+            field_out.at[slots[k]], field_in.at[slots[k]], field_send, field_recv.at[k],
+            device_id=partner, device_id_type=MESH,
+        ).start()
 
     charges_copy.wait()
     q = [charges_ref[side * (NS - 2 * t) + t].astype(jnp.float32) for t in range(NS + 1)]
@@ -179,7 +169,7 @@
 
     def begin_chain(chain, x):
         for h in range(parts):
-            value = start_v[x, :, plane(h)] if chain == OWN else read_log(field_in[x, h], 0)
+            value = start_v[x, :, plane(h)] if chain == OWN else read_log(field_in[slot_of[x], h], 0)
             u[chain, 0, x + 2, h] = factor[index(chain, 0), x + 1, h] * value
             rounded[chain, 0, x, h] = to_bfloat16(value)
 
@@ -223,6 +213,9 @@
     def outer(step):
         loop(0, 2, lambda k: step((layers - 1) * k))
 
+    def ring(first, step):
+        loop(0, 2, lambda k: step(first + (layers - 1 - 2 * first) * k))
+
     def beyond(step):
         loop(0, 2, lambda k: step((layers + 1) * k - 1))
 
@@ -235,8 +228,9 @@
     def in_layer(d, j):
         return -1 - j if d else layers + j
 
-    for copy in local:
-        copy.wait()
+    taken(w_v.at[pl.ds(1, layers)], local_sem.at[0])
+    taken(psi_v.at[pl.ds(2, layers)], local_sem.at[1])
+    taken(start_v, local_sem.at[2])
     for d in (0, 1):
         edge_pair(d, make_factor)
         edge_pair(d, functools.partial(begin_chain, OWN))
@@ -252,20 +246,18 @@
     edges = [
         pltpu.make_async_remote_copy(
             edge_out.at[d, pl.ds(first, count)], edge_in.at[d, pl.ds(first, count)],
-            edge_send.at[d, n], edge_recv.at[d, n], device_id=targets[d], device_id_type=MESH,
+            edge_send, edge_recv.at[n], device_id=targets[d], device_id_type=MESH,
         )
         for n, (first, count) in enumerate(((0, 4), (4, 1))) for d in (0, 1)
     ]
-    sent += edges
-
-    def send_edges(seam):
-        for d in (0, 1):
-            @pl.when(seams[d] if seam else jnp.logical_not(seams[d]))
-            def _(d=d):
-                edges[d].start()
-                edges[2 + d].start()
-
-    send_edges(False)
+
+    @pl.when(jnp.logical_not(first_slab))
+    def _():
+        edges[0].start()
+        edges[2].start()
+
+    edges[1].start()
+    edges[3].start()
     stages = len(near)
 
     def open_gate(stage):
@@ -282,7 +274,6 @@
     pass_gate(0)
     adv(OWN, 0, 1, layers - 1)
     adv(OWN, 1, 2, layers - 2)
-    pass_gate(1)
     adv(OWN, 2, 3, layers - 3)
 
     def relaxation(center, total):
@@ -294,33 +285,35 @@
             total = psi_v[x + 1, h, window] + psi_v[x + 3, h, window] + sums[h]
             base[x + 1, h] = relaxation(center[h], total)
 
+    @pl.when(first_slab)
+    def _():
+        pl.semaphore_wait(seam_gate, 1)
+        edges[0].start()
+        edges[2].start()
+
     loop(1, layers - 1, make_base)
-    for stage in range(2, stages - 1):
-        pass_gate(stage)
-    send_edges(True)
+    pass_gate(1)
 
     def halo(kind, d, first, count):
         return pltpu.make_async_remote_copy(
             halo_out.at[kind, d, pl.ds(first, count)], halo_in.at[kind, d, pl.ds(first, count)],
-            halo_send.at[kind, d, first], halo_recv.at[kind, d, first],
+            halo_send, halo_recv.at[kind],
             device_id=targets[d], device_id_type=MESH,
         )
 
     def arrive(group):
-        for x in groups[group]:
-            fields[x].wait_recv()
+        taken(field_in.at[slots[group]], field_recv.at[group])
         for x in groups[group]:
             begin_chain(FOREIGN, x)
 
-    copies = []
     for j in (0, 1):
         arrive(j)
         for d in (0, 1):
             halo_out[0, d, j] = write_log(u[FOREIGN, 0, out_layer(d, j) + 2], 1)
-            copies.append(send(halo(0, d, j, 1)))
-
-    for copy in edges[:2]:
-        copy.wait_recv()
+            halo(0, d, j, 1).start()
+
+    pass_gate(2)
+    taken(edge_in.at[:, pl.ds(0, 4)], edge_recv.at[0])
     for d in (0, 1):
         x = in_layer(d, 0)
         for h in range(parts):
@@ -333,42 +326,36 @@
     outer(functools.partial(advance, OWN, 0))
 
     def half_way(chain, kind):
-        result = []
         for d in (0, 1):
             edge_pair(d, functools.partial(advance, chain, 1))
             for j in (0, 1):
                 halo_out[kind, d, j] = write_log(u[chain, 2, out_layer(d, j) + 2], 5)
-            result.append(send(halo(kind, d, 0, 2)))
-        return result
-
-    own_copies = half_way(OWN, 1)
-    adv(OWN, 2, 1, 3)
-    adv(OWN, 2, layers - 3, layers - 1)
-    adv(OWN, 3, 2, layers - 2)
-
+            halo(kind, d, 0, 2).start()
+
+    half_way(OWN, 1)
     arrive(2)
-    adv(FOREIGN, 0, 1, 2)
-    adv(FOREIGN, 0, layers - 2, layers - 1)
+    ring(1, functools.partial(advance, FOREIGN, 0))
     arrive(3)
-    adv(FOREIGN, 0, 2, layers - 2)
-    adv(FOREIGN, 1, 2, layers - 2)
-    adv(FOREIGN, 2, 3, layers - 3)
-    for copy in copies:
-        copy.wait_recv()
+    ring(2, functools.partial(advance, FOREIGN, 0))
+    taken(halo_in.at[0], halo_recv.at[0])
     for d in (0, 1):
         for j in (0, 1):
             u[FOREIGN, 0, in_layer(d, j) + 2] = read_log(halo_in[0, d, j], 1)
     beyond(functools.partial(advance_halo, FOREIGN, 0))
     outer(functools.partial(advance, FOREIGN, 0))
-    foreign_copies = half_way(FOREIGN, 2)
-
-    pass_gate(stages - 1)
-    adv(FOREIGN, 2, 1, 3)
-    adv(FOREIGN, 2, layers - 3, layers - 1)
-
-    def second_half(chain, kind, copies):
-        for copy in copies:
-            copy.wait_recv()
+    half_way(FOREIGN, 2)
+
+    adv(FOREIGN, 0, 3, layers - 3)
+    for stage in range(3, stages - 1):
+        pass_gate(stage)
+    adv(OWN, 2, 1, 3)
+    adv(OWN, 2, layers - 3, layers - 1)
+    adv(OWN, 3, 2, layers - 2)
+    adv(FOREIGN, 1, 2, layers - 2)
+    adv(FOREIGN, 2, 1, layers - 1)
+
+    def second_half(chain, kind):
+        taken(halo_in.at[kind], halo_recv.at[kind])
         for d in (0, 1):
             for j in (0, 1):
                 u[chain, 2, in_layer(d, j) + 2] = read_log(halo_in[kind, d, j], 5)
@@ -407,7 +394,8 @@
 
     loop(2, layers - 2, whole)
 
-    second_half(OWN, 1, own_copies)
+    pass_gate(stages - 1)
+    second_half(OWN, 1)
     for d in (0, 1):
         edge_pair(d, functools.partial(advance, OWN, 3))
 
@@ -419,37 +407,39 @@
     for d in (0, 1):
         edge_pair(d, gather)
 
-    for copy in edges[2:]:
-        copy.wait_recv()
+    taken(edge_in.at[:, pl.ds(4, 1)], edge_recv.at[1])
     for d in (0, 1):
         psi_v[in_layer(d, 1) + 2] = read_code(edge_in[d, 4], *psi_span)
     for k in (-1, 0):
         make_base(k)
         make_base(layers - 1 - k)
 
-    second_half(FOREIGN, 2, foreign_copies)
-    rho_copies = []
+    steps = sorted(range(1, devices), key=lambda k: -min(k % slabs, slabs - k % slabs))
+    receivers = [(k, device(k)) for k in steps] if devices <= 32 else None
+    second_half(FOREIGN, 2)
     for d in (0, 1):
         edge_pair(d, finish)
         rho_out[d] = rho[out_layer(d, 0) + 1].astype(jnp.bfloat16)
-        rho_copies.append(send(pltpu.make_async_remote_copy(
-            rho_out.at[d], rho_in.at[d], rho_send.at[d], rho_recv.at[d], device_id=targets[d], device_id_type=MESH,
-        )))
+        pltpu.make_async_remote_copy(
+            rho_out.at[d], rho_in.at[d], rho_send, rho_recv, device_id=targets[d], device_id_type=MESH,
+        ).start()
     for x in (0, 1, layers - 2, layers - 1):
         partial = partial + cells_of(x)
     sums[0] = jnp.sum(partial, axis=0, keepdims=True)
 
-    def share(step, carry):
+    def share(step, target):
         pltpu.make_async_remote_copy(
-            sums.at[0], sums.at[step], sum_send, sum_recv,
-            device_id=device(step), device_id_type=MESH,
+            sums.at[0], sums.at[step], sum_send, sum_recv, device_id=target, device_id_type=MESH,
         ).start()
-        return carry
-
-    lax.fori_loop(1, devices, share, 0)
+
+    if receivers is not None:
+        for step, target in receivers:
+            share(step, target)
+    else:
+        lax.fori_loop(1, devices, lambda step, carry: (share(step, device(step)), carry)[1], 0)
 
     others = sums.at[pl.ds(1, devices - 1)]
-    pltpu.make_async_copy(others, others, sum_recv).wait()
+    taken(others, sum_recv)
     cells = float(devices * layers * half * w_hbm.shape[2])
     inverse = cells / jnp.sum(sums[...])
     scaled = inverse * (1.0 / (6.0 + screening))
@@ -473,20 +463,31 @@
             potential_ref[x, :, h * LANES:(h + 1) * LANES] = value
 
     loop(1, layers - 1, second)
-    for copy in rho_copies:
-        copy.wait_recv()
+    taken(rho_in, rho_recv)
     for d in (0, 1):
         rho[in_layer(d, 0) + 1] = rho_in[d].astype(jnp.float32)
         relax_once(in_layer(d, 0))
     outer(second)
 
-    for copy in sent:
-        copy.wait_send()
-    pltpu.make_async_copy(others, others, sum_send).wait()
+    for ref, semaphore in (
+        (field_out, field_send), (edge_out, edge_send), (halo_out, halo_send), (rho_out, rho_send), (others, sum_send)
+    ):
+        taken(ref, semaphore)
 
 
 def ion_charge(value):
     return (2.0 * screening) * jnp.tanh(0.5 * value)
+
+
+def store(density_v, potential_v, density_hbm, potential_hbm, sems):
+    copies = [
+        pltpu.make_async_copy(source, target, sems.at[k])
+        for k, (source, target) in enumerate(((density_v, density_hbm), (potential_v, potential_hbm)))
+    ]
+    for copy in copies:
+        copy.start()
+    for copy in copies:
+        copy.wait()
 
 
 def body(ends, slabs, w_field, psi_init, start_field, charges):
@@ -517,7 +518,7 @@
 
     hbm = pl.BlockSpec(memory_space=pltpu.HBM)
     vmem = pl.BlockSpec(memory_space=pltpu.VMEM)
-    return pl.pallas_call(
+    density, potential = pl.pallas_call(
         functools.partial(kernel, ends, slabs),
         out_shape=(out, out),
         in_specs=[hbm, hbm, hbm, hbm],
@@ -528,14 +529,22 @@
             slim(layers), slim(layers + 2), slim(layers + 2), slim(layers + 2),
             pltpu.VMEM((devices, 1, LANES), jnp.float32),
             code(layers), code(layers), code(2, 5), code(2, 5), code(3, 2, 2), code(3, 2, 2), edge_rho, edge_rho,
-            pltpu.SemaphoreType.REGULAR((stages,)), dma(()), dma((layers, 3)), dma((2 + parts, 3)), dma((layers,)), dma((layers,)),
-            dma((2, 2)), dma((2, 2)), dma((3, 2, 2)), dma((3, 2, 2)), dma((2,)), dma((2,)), dma(()), dma(()),
+            pltpu.SemaphoreType.REGULAR((stages,)), pltpu.SemaphoreType.REGULAR, dma(()), dma((4,)), dma((3,)), dma(()), dma((4,)),
+            dma(()), dma((2,)), dma(()), dma((3,)), dma(()), dma(()), dma(()), dma(()),
         ],
         compiler_params=pltpu.CompilerParams(
             collective_id=0, has_side_effects=True, vmem_limit_bytes=40 * 1024 * 1024
         ),
         name="scf_step",
     )(*[pltpu.with_memory_space_constraint(v, pltpu.HBM) for v in (charges, w_field, psi_init, start_field)])
+    return pl.pallas_call(
+        store,
+        out_shape=(out, out),
+        in_specs=[pl.BlockSpec(memory_space=pl.ANY)] * 2,
+        out_specs=(hbm, hbm),
+        scratch_shapes=[dma((2,))],
+        name="store",
+    )(*[pltpu.with_memory_space_constraint(v, pltpu.VMEM) for v in (density, potential)])
 
 
 def solution(mesh):

time: 30 us -> 27.3 us (0.910)
  local copies, waits for them, and re-layouts: 1.59 us -> 0 us
  Pallas kernels: 27.6 us -> 26.5 us
    pallas_call x1, Pallas kernels: 27.6 us -> 25.5 us  [body(): pl.pallas_call(functools.partial(kernel, ends, slabs), out_shape=(out, ou...]
    unnamed x2 -> x0, local copies, waits for them, and re-layouts: 1.59 us -> none
    pallas_call x0 -> x1, Pallas kernels: none -> 0.99 us  [body(): pl.pallas_call(store, out_shape=(out, out), in_specs=[pl.BlockSpec(memory...]
where the time goes in v5:
time: 27.3 us; the launch traced here: 27.1 us
  Pallas kernels  26.5 us (97%)
  between operations  0.64 us (2%)
    pallas_call x1, Pallas kernels, body(): pl.pallas_call(functools.partial(kernel, ends, slabs), out_shape=(out, ou...  25.5 us
    pallas_call x1, Pallas kernels, body(): pl.pallas_call(store, out_shape=(out, out), in_specs=[pl.BlockSpec(memory...  0.99 us

profile of v5, /device:TPU:0, one launch (start us, length us, event | category | flops | bytes accessed | tf_op | source)
XLA Modules:
  0.0 27.1 jit_solution(6951164328284941383)
XLA Ops:
  0.6 25.5 %scf_step.1 = (f32[8,64,256]{2,1,0:T(8,128)S(1)}, f32[8,64,256]{2,1,0:T(8,128)S(1)}) custom-call(s32[5]{0:T(128)} %charges_hbm.1, f32[8,128,256]{2,1,0:T(8,128)} %w_hbm.1, f32[8,128,256]{2,1,0:T(8,128)} %psi_hbm.1, f32[1,8,128,256]{3,2,1,0:T(8,128)} %start_hbm.1), custom_call_target="tpu_custom_call" | custom-call | tf_op jit(solution)/shard_map/scf_step/pallas_call | solution.py:521
  26.1 1.0 %store.1 = (f32[8,64,256]{2,1,0:T(8,128)}, f32[8,64,256]{2,1,0:T(8,128)}) custom-call(f32[8,64,256]{2,1,0:T(8,128)S(1)} %get-tuple-element.4.density_v, f32[8,64,256]{2,1,0:T(8,128)S(1)} %get-tuple-element.5.potential_v), custom_call_target="tpu_custom_call" | custom-call | tf_op jit(solution)/shard_map/store/pallas_call | solution.py:540

commit v6 on v5

--- a/solution.py
+++ b/solution.py
@@ -294,11 +294,17 @@
     loop(1, layers - 1, make_base)
     pass_gate(1)
 
+    def neighbour_of(d):
+        return (side, lax.rem(slab + slabs + 2 * d - 1, slabs))
+
+    def edge(d, k):
+        return d * (layers - 1) + k * (1 - 2 * d)
+
     def halo(kind, d, first, count):
         return pltpu.make_async_remote_copy(
             halo_out.at[kind, d, pl.ds(first, count)], halo_in.at[kind, d, pl.ds(first, count)],
-            halo_send, halo_recv.at[kind],
-            device_id=targets[d], device_id_type=MESH,
+            halo_send, halo_recv.at[kind, d],
+            device_id=neighbour_of(d), device_id_type=MESH,
         )
 
     def arrive(group):
@@ -337,13 +343,19 @@
     ring(1, functools.partial(advance, FOREIGN, 0))
     arrive(3)
     ring(2, functools.partial(advance, FOREIGN, 0))
-    taken(halo_in.at[0], halo_recv.at[0])
-    for d in (0, 1):
+    sides = (1 - slab % 2, slab % 2)
+    first_side = jnp.where(slab % (slabs - 1) == 0, sides[0], sides[1])
+    for d in (first_side, 1 - first_side):
+        taken(halo_in.at[0, 1 - d], halo_recv.at[0, 1 - d])
         for j in (0, 1):
-            u[FOREIGN, 0, in_layer(d, j) + 2] = read_log(halo_in[0, d, j], 1)
-    beyond(functools.partial(advance_halo, FOREIGN, 0))
-    outer(functools.partial(advance, FOREIGN, 0))
-    half_way(FOREIGN, 2)
+            u[FOREIGN, 0, edge(d, -1 - j) + 2] = read_log(halo_in[0, 1 - d, j], 1)
+        advance_halo(FOREIGN, 0, edge(d, -1))
+        for j in (0,):
+            advance(FOREIGN, 0, edge(d, j))
+        for j in (0, 1):
+            advance(FOREIGN, 1, edge(d, j))
+            halo_out[2, d, j] = write_log(u[FOREIGN, 2, edge(d, j) + 2], 5)
+        halo(2, d, 0, 2).start()
 
     adv(FOREIGN, 0, 3, layers - 3)
     for stage in range(3, stages - 1):
@@ -355,8 +367,8 @@
     adv(FOREIGN, 2, 1, layers - 1)
 
     def second_half(chain, kind):
-        taken(halo_in.at[kind], halo_recv.at[kind])
         for d in (0, 1):
+            taken(halo_in.at[kind, d], halo_recv.at[kind, d])
             for j in (0, 1):
                 u[chain, 2, in_layer(d, j) + 2] = read_log(halo_in[kind, d, j], 5)
         beyond(functools.partial(advance_halo, chain, 2))
@@ -414,17 +426,30 @@
         make_base(k)
         make_base(layers - 1 - k)
 
-    steps = sorted(range(1, devices), key=lambda k: -min(k % slabs, slabs - k % slabs))
-    receivers = [(k, device(k)) for k in steps] if devices <= 32 else None
-    second_half(FOREIGN, 2)
-    for d in (0, 1):
-        edge_pair(d, finish)
-        rho_out[d] = rho[out_layer(d, 0) + 1].astype(jnp.bfloat16)
+    bits = [1 << k for k in range(slabs.bit_length() - 1)]
+    flips = [bit - 2 * bit * lax.rem(slab // bit, 2) for bit in bits]
+
+    def mirror(mask):
+        target = slab
+        for bit, flip in zip(bits, flips):
+            target = target + flip if mask & bit else target
+        return (other if mask >= slabs else side, target)
+
+    masks = sorted(range(1, devices), key=lambda mask: (-(mask % slabs // 4), -mask))
+    receivers = [(mask, mirror(mask)) for mask in masks] if ends == 2 and devices <= 32 else None
+    for d in sides:
+        taken(halo_in.at[2, 1 - d], halo_recv.at[2, 1 - d])
+        for j in (0, 1):
+            u[FOREIGN, 2, edge(d, -1 - j) + 2] = read_log(halo_in[2, 1 - d, j], 5)
+        advance_halo(FOREIGN, 2, edge(d, -1))
+        advance(FOREIGN, 2, edge(d, 0))
+        finish(edge(d, 0))
+        rho_out[d] = rho[edge(d, 0) + 1].astype(jnp.bfloat16)
         pltpu.make_async_remote_copy(
-            rho_out.at[d], rho_in.at[d], rho_send, rho_recv, device_id=targets[d], device_id_type=MESH,
+            rho_out.at[d], rho_in.at[d], rho_send, rho_recv, device_id=neighbour_of(d), device_id_type=MESH,
         ).start()
-    for x in (0, 1, layers - 2, layers - 1):
-        partial = partial + cells_of(x)
+        finish(edge(d, 1))
+        partial = partial + cells_of(edge(d, 0)) + cells_of(edge(d, 1))
     sums[0] = jnp.sum(partial, axis=0, keepdims=True)
 
     def share(step, target):
@@ -439,6 +464,9 @@
         lax.fori_loop(1, devices, lambda step, carry: (share(step, device(step)), carry)[1], 0)
 
     others = sums.at[pl.ds(1, devices - 1)]
+    taken(rho_in, rho_recv)
+    for d in (0, 1):
+        rho[in_layer(d, 0) + 1] = rho_in[d].astype(jnp.float32)
     taken(others, sum_recv)
     cells = float(devices * layers * half * w_hbm.shape[2])
     inverse = cells / jnp.sum(sums[...])
@@ -451,9 +479,7 @@
     def first(x):
         for h in range(parts):
             density_ref[x, :, h * LANES:(h + 1) * LANES] = phi[x, h, inner] * inverse
-        relax_once(x)
-
-    loop(0, layers, first)
+    loop(-1, layers + 1, relax_once)
 
     def second(x):
         center, sums = around(relaxed, (x + 1,), PAD - EDGE, half)
@@ -462,12 +488,8 @@
             value = relaxation(center[h], total) + rho[x + 1, h, inner] * scaled
             potential_ref[x, :, h * LANES:(h + 1) * LANES] = value
 
-    loop(1, layers - 1, second)
-    taken(rho_in, rho_recv)
-    for d in (0, 1):
-        rho[in_layer(d, 0) + 1] = rho_in[d].astype(jnp.float32)
-        relax_once(in_layer(d, 0))
-    outer(second)
+    loop(0, layers, second)
+    loop(0, layers, first)
 
     for ref, semaphore in (
         (field_out, field_send), (edge_out, edge_send), (halo_out, halo_send), (rho_out, rho_send), (others, sum_send)
@@ -530,7 +552,7 @@
             pltpu.VMEM((devices, 1, LANES), jnp.float32),
             code(layers), code(layers), code(2, 5), code(2, 5), code(3, 2, 2), code(3, 2, 2), edge_rho, edge_rho,
             pltpu.SemaphoreType.REGULAR((stages,)), pltpu.SemaphoreType.REGULAR, dma(()), dma((4,)), dma((3,)), dma(()), dma((4,)),
-            dma(()), dma((2,)), dma(()), dma((3,)), dma(()), dma(()), dma(()), dma(()),
+            dma(()), dma((2,)), dma(()), dma((3, 2)), dma(()), dma(()), dma(()), dma(()),
         ],
         compiler_params=pltpu.CompilerParams(
             collective_id=0, has_side_effects=True, vmem_limit_bytes=40 * 1024 * 1024

time: 27.3 us -> 27 us (0.989)
  Pallas kernels: 26.5 us -> 26.2 us
where the time goes in v6:
time: 27 us; the launch traced here: 26.9 us
  Pallas kernels  26.2 us (97%)
  between operations  0.64 us (2%)
    pallas_call x1, Pallas kernels, body(): pl.pallas_call(functools.partial(kernel, ends, slabs), out_shape=(out, ou...  25.3 us
    pallas_call x1, Pallas kernels, body(): pl.pallas_call(store, out_shape=(out, out), in_specs=[pl.BlockSpec(memory...  0.99 us

profile of v6, /device:TPU:0, one launch (start us, length us, event | category | flops | bytes accessed | tf_op | source)
XLA Modules:
  0.0 26.9 jit_solution(10096624385545834475)
XLA Ops:
  0.6 25.3 %scf_step.1 = (f32[8,64,256]{2,1,0:T(8,128)S(1)}, f32[8,64,256]{2,1,0:T(8,128)S(1)}) custom-call(s32[5]{0:T(128)} %charges_hbm.1, f32[8,128,256]{2,1,0:T(8,128)} %w_hbm.1, f32[8,128,256]{2,1,0:T(8,128)} %psi_hbm.1, f32[1,8,128,256]{3,2,1,0:T(8,128)} %start_hbm.1), custom_call_target="tpu_custom_call" | custom-call | tf_op jit(solution)/shard_map/scf_step/pallas_call | solution.py:543
  25.9 1.0 %store.1 = (f32[8,64,256]{2,1,0:T(8,128)}, f32[8,64,256]{2,1,0:T(8,128)}) custom-call(f32[8,64,256]{2,1,0:T(8,128)S(1)} %get-tuple-element.4.density_v, f32[8,64,256]{2,1,0:T(8,128)S(1)} %get-tuple-element.5.potential_v), custom_call_target="tpu_custom_call" | custom-call | tf_op jit(solution)/shard_map/store/pallas_call | solution.py:562

commit v7 on v6

--- a/solution.py
+++ b/solution.py
@@ -12,6 +12,7 @@
 PAD = 8
 EDGE = 4
 LANES = 128
+CHUNK = 4
 mobility = 0.15
 screening = 1.0
 OWN, FOREIGN = 0, 1
@@ -22,8 +23,8 @@
 MESH = pl.DeviceIdType.MESH
 
 
-def kernel(ends, slabs, charges_hbm, w_hbm, psi_hbm, start_hbm, density_ref, potential_ref,
-           charges_ref, w_v, psi_v, start_v, theirs_v, factor, u, rounded, phi, rho, base, relaxed, sums,
+def kernel(ends, slabs, charges_hbm, w_hbm, psi_hbm, start_hbm, phi, rho, base, scale_ref,
+           charges_ref, w_v, psi_v, start_v, theirs_v, factor, u, rounded, sums,
            field_out, field_in, edge_out, edge_in, halo_out, halo_in, rho_out, rho_in,
            gate, seam_gate, charges_sem, field_sem, local_sem, field_send, field_recv, edge_send, edge_recv, halo_send, halo_recv,
            rho_send, rho_recv, sum_send, sum_recv):
@@ -130,6 +131,13 @@
     def plane(h):
         return slice(h * LANES, (h + 1) * LANES)
 
+    def field(k):
+        return pltpu.make_async_remote_copy(
+            field_out.at[slots[k]], field_in.at[slots[k]], field_send, field_recv.at[k],
+            device_id=partner, device_id_type=MESH,
+        )
+
+    holds_back = slab % 2 == 1
     for k, group in enumerate(groups):
         taken(theirs_v.at[slots[k]], field_sem.at[k])
         for x in group:
@@ -142,10 +150,12 @@
             def _():
                 pl.semaphore_signal(seam_gate, inc=1, device_id=right, device_id_type=MESH)
 
-        pltpu.make_async_remote_copy(
-            field_out.at[slots[k]], field_in.at[slots[k]], field_send, field_recv.at[k],
-            device_id=partner, device_id_type=MESH,
-        ).start()
+        if k < 2:
+            field(k).start()
+        else:
+            @pl.when(jnp.logical_not(holds_back))
+            def _(k=k):
+                field(k).start()
 
     charges_copy.wait()
     q = [charges_ref[side * (NS - 2 * t) + t].astype(jnp.float32) for t in range(NS + 1)]
@@ -172,20 +182,6 @@
             value = start_v[x, :, plane(h)] if chain == OWN else read_log(field_in[slot_of[x], h], 0)
             u[chain, 0, x + 2, h] = factor[index(chain, 0), x + 1, h] * value
             rounded[chain, 0, x, h] = to_bfloat16(value)
-
-    lane = lax.broadcasted_iota(jnp.int32, (1, LANES), 1)
-    lowest, highest = lane == 0, lane == LANES - 1
-
-    def around(ref, at, first, count):
-        center = [ref[(*at, h, pl.ds(first, count))] for h in range(parts)]
-        lower = [pltpu.roll(value, 1, 1) for value in center]
-        upper = [pltpu.roll(value, LANES - 1, 1) for value in center]
-        sums = []
-        for h in range(parts):
-            total = ref[(*at, h, pl.ds(first - 1, count))] + ref[(*at, h, pl.ds(first + 1, count))]
-            total = total + jnp.where(lowest, lower[h - 1], lower[h])
-            sums.append(total + jnp.where(highest, upper[(h + 1) % parts], upper[h]))
-        return center, sums
 
     def advanced(chain, t, x):
         center, sums = around(u, (chain, t, x + 2), EDGE, window.size)
@@ -254,10 +250,8 @@
     @pl.when(jnp.logical_not(first_slab))
     def _():
         edges[0].start()
-        edges[2].start()
 
     edges[1].start()
-    edges[3].start()
     stages = len(near)
 
     def open_gate(stage):
@@ -276,8 +270,11 @@
     adv(OWN, 1, 2, layers - 2)
     adv(OWN, 2, 3, layers - 3)
 
-    def relaxation(center, total):
-        return (total - ion_charge(center) + screening * center) * (1.0 / (6.0 + screening))
+    @pl.when(holds_back)
+    def _():
+        field(2).start()
+        field(3).start()
+
 
     def make_base(x):
         center, sums = around(psi_v, (x + 2,), EDGE, window.size)
@@ -289,7 +286,6 @@
     def _():
         pl.semaphore_wait(seam_gate, 1)
         edges[0].start()
-        edges[2].start()
 
     loop(1, layers - 1, make_base)
     pass_gate(1)
@@ -317,6 +313,8 @@
         for d in (0, 1):
             halo_out[0, d, j] = write_log(u[FOREIGN, 0, out_layer(d, j) + 2], 1)
             halo(0, d, j, 1).start()
+    edges[2].start()
+    edges[3].start()
 
     pass_gate(2)
     taken(edge_in.at[:, pl.ds(0, 4)], edge_recv.at[0])
@@ -470,26 +468,7 @@
     taken(others, sum_recv)
     cells = float(devices * layers * half * w_hbm.shape[2])
     inverse = cells / jnp.sum(sums[...])
-    scaled = inverse * (1.0 / (6.0 + screening))
-
-    def relax_once(x):
-        for h in range(parts):
-            relaxed[x + 1, h] = base[x + 1, h] + rho[x + 1, h] * scaled
-
-    def first(x):
-        for h in range(parts):
-            density_ref[x, :, h * LANES:(h + 1) * LANES] = phi[x, h, inner] * inverse
-    loop(-1, layers + 1, relax_once)
-
-    def second(x):
-        center, sums = around(relaxed, (x + 1,), PAD - EDGE, half)
-        for h in range(parts):
-            total = relaxed[x, h, inner] + relaxed[x + 2, h, inner] + sums[h]
-            value = relaxation(center[h], total) + rho[x + 1, h, inner] * scaled
-            potential_ref[x, :, h * LANES:(h + 1) * LANES] = value
-
-    loop(0, layers, second)
-    loop(0, layers, first)
+    scale_ref[...] = jnp.broadcast_to(inverse, scale_ref.shape)
 
     for ref, semaphore in (
         (field_out, field_send), (edge_out, edge_send), (halo_out, halo_send), (rho_out, rho_send), (others, sum_send)
@@ -501,15 +480,52 @@
     return (2.0 * screening) * jnp.tanh(0.5 * value)
 
 
-def store(density_v, potential_v, density_hbm, potential_hbm, sems):
-    copies = [
-        pltpu.make_async_copy(source, target, sems.at[k])
-        for k, (source, target) in enumerate(((density_v, density_hbm), (potential_v, potential_hbm)))
-    ]
-    for copy in copies:
-        copy.start()
-    for copy in copies:
-        copy.wait()
+def relaxation(center, total):
+    return (total - ion_charge(center) + screening * center) * (1.0 / (6.0 + screening))
+
+
+def around(ref, at, first, count):
+    parts = ref.shape[-3]
+    lane = lax.broadcasted_iota(jnp.int32, (1, LANES), 1)
+    lowest, highest = lane == 0, lane == LANES - 1
+    center = [ref[(*at, h, pl.ds(first, count))] for h in range(parts)]
+    lower = [pltpu.roll(value, 1, 1) for value in center]
+    upper = [pltpu.roll(value, LANES - 1, 1) for value in center]
+    sums = []
+    for h in range(parts):
+        total = ref[(*at, h, pl.ds(first - 1, count))] + ref[(*at, h, pl.ds(first + 1, count))]
+        total = total + jnp.where(lowest, lower[h - 1], lower[h])
+        sums.append(total + jnp.where(highest, upper[(h + 1) % parts], upper[h]))
+    return center, sums
+
+
+def finishing(phi, rho, base, scale_ref, density_hbm, potential_hbm, density, potential, relaxed, density_sem, potential_sem):
+    layers, half = density_hbm.shape[0], density_hbm.shape[1]
+    parts = phi.shape[1]
+    inner = pl.ds(PAD - EDGE, half)
+    inverse = scale_ref[...]
+    scaled = inverse * (1.0 / (6.0 + screening))
+
+    def plane(h):
+        return slice(h * LANES, (h + 1) * LANES)
+
+    for x in range(layers):
+        for h in range(parts):
+            density[x, :, plane(h)] = phi[x, h, inner] * inverse
+    pltpu.make_async_copy(density, density_hbm, density_sem).start()
+    for x in range(layers + 2):
+        for h in range(parts):
+            relaxed[x, h] = base[x, h] + rho[x, h] * scaled
+    for x in range(layers):
+        center, sums = around(relaxed, (x + 1,), PAD - EDGE, half)
+        for h in range(parts):
+            total = relaxed[x, h, inner] + relaxed[x + 2, h, inner] + sums[h]
+            potential[x, :, plane(h)] = relaxation(center[h], total) + rho[x + 1, h, inner] * scaled
+        if x % CHUNK == CHUNK - 1:
+            done = pl.ds(x + 1 - CHUNK, CHUNK)
+            pltpu.make_async_copy(potential.at[done], potential_hbm.at[done], potential_sem).start()
+    pltpu.make_async_copy(density, density_hbm, density_sem).wait()
+    pltpu.make_async_copy(potential, potential_hbm, potential_sem).wait()
 
 
 def body(ends, slabs, w_field, psi_init, start_field, charges):
@@ -540,15 +556,17 @@
 
     hbm = pl.BlockSpec(memory_space=pltpu.HBM)
     vmem = pl.BlockSpec(memory_space=pltpu.VMEM)
-    density, potential = pl.pallas_call(
+    def planes(count):
+        return jax.ShapeDtypeStruct((count, parts, narrow, LANES), jnp.float32)
+
+    fields = pl.pallas_call(
         functools.partial(kernel, ends, slabs),
-        out_shape=(out, out),
+        out_shape=(planes(layers), planes(layers + 2), planes(layers + 2), jax.ShapeDtypeStruct((1, LANES), jnp.float32)),
         in_specs=[hbm, hbm, hbm, hbm],
-        out_specs=(vmem, vmem),
+        out_specs=(vmem, vmem, vmem, vmem),
         scratch_shapes=[
             pltpu.SMEM((NS + 1,), jnp.int32), whole_rows(layers + 2), tile(layers + 4), whole_rows(layers), whole_rows(layers),
             tile(NS, layers + 2), tile(2, NS, layers + 4), tile(2, NS + 1, layers),
-            slim(layers), slim(layers + 2), slim(layers + 2), slim(layers + 2),
             pltpu.VMEM((devices, 1, LANES), jnp.float32),
             code(layers), code(layers), code(2, 5), code(2, 5), code(3, 2, 2), code(3, 2, 2), edge_rho, edge_rho,
             pltpu.SemaphoreType.REGULAR((stages,)), pltpu.SemaphoreType.REGULAR, dma(()), dma((4,)), dma((3,)), dma(()), dma((4,)),
@@ -559,14 +577,15 @@
         ),
         name="scf_step",
     )(*[pltpu.with_memory_space_constraint(v, pltpu.HBM) for v in (charges, w_field, psi_init, start_field)])
+    result = pltpu.VMEM((layers, half, depth), jnp.float32)
     return pl.pallas_call(
-        store,
+        finishing,
         out_shape=(out, out),
-        in_specs=[pl.BlockSpec(memory_space=pl.ANY)] * 2,
+        in_specs=[vmem] * 4,
         out_specs=(hbm, hbm),
-        scratch_shapes=[dma((2,))],
-        name="store",
-    )(*[pltpu.with_memory_space_constraint(v, pltpu.VMEM) for v in (density, potential)])
+        scratch_shapes=[result, result, slim(layers + 2), dma(()), dma(())],
+        name="finishing",
+    )(*[pltpu.with_memory_space_constraint(v, pltpu.VMEM) for v in fields])
 
 
 def solution(mesh):

time: 27 us -> 26.7 us (0.989)
  Pallas kernels: 26.2 us -> 25.9 us
    pallas_call x2, Pallas kernels: 26.2 us -> 25.9 us  [the longest x1 24.5 us: body(): pl.pallas_call(functools.partial(kernel, ends, slabs), out_shape=(planes(...]
where the time goes in v7:
time: 26.7 us; the launch traced here: 26.5 us
  Pallas kernels  25.9 us (97%)
  between operations  0.64 us (2%)
    pallas_call x1, Pallas kernels, body(): pl.pallas_call(functools.partial(kernel, ends, slabs), out_shape=(planes(...  24.5 us
    pallas_call x1, Pallas kernels, body(): pl.pallas_call(finishing, out_shape=(out, out), in_specs=[vmem] * 4, out_...  1.34 us

profile of v7, /device:TPU:0, one launch (start us, length us, event | category | flops | bytes accessed | tf_op | source)
XLA Modules:
  0.0 26.5 jit_solution(12244214454794815103)
XLA Ops:
  0.6 24.5 %scf_step.1 = (f32[8,2,72,128]{3,2,1,0:T(8,128)S(1)}, f32[10,2,72,128]{3,2,1,0:T(8,128)S(1)}, f32[10,2,72,128]{3,2,1,0:T(8,128)S(1)}, f32[1,128]{1,0:T(1,128)S(1)}) custom-call(s32[5]{0:T(128)} %charges_hbm.1, f32[8,128,256]{2,1,0:T(8,128)} %w_hbm.1, f32[8,128,256]{2,1,0:T(8,128)} %psi_hbm.1, f32[1,8,128,256]{3,2,1,0:T(8,128)} %start_hbm.1), custom_call_target="tpu_custom_call" | custom-call | tf_op jit(solution)/shard_map/scf_step/pallas_call | solution.py:562
  25.2 1.3 %finishing.1 = (f32[8,64,256]{2,1,0:T(8,128)}, f32[8,64,256]{2,1,0:T(8,128)}) custom-call(f32[8,2,72,128]{3,2,1,0:T(8,128)S(1)} %get-tuple-element.6.phi, f32[10,2,72,128]{3,2,1,0:T(8,128)S(1)} %get-tuple-element.7.rho, f32[10,2,72,128]{3,2,1,0:T(8,128)S(1)} %get-tuple-element.8.base, f32[1,128]{1,0:T(1,128)S(1)} %get-tuple-element.9.scale_ref), custom_call_target="tpu_custom_call" | custom-call | tf_op jit(solution)/shard_map/finishing/pallas_call | solution.py:581

commit v8 on v7

--- a/solution.py
+++ b/solution.py
@@ -137,25 +137,20 @@
             device_id=partner, device_id_type=MESH,
         )
 
-    holds_back = slab % 2 == 1
-    for k, group in enumerate(groups):
+    def code_group(k):
         taken(theirs_v.at[slots[k]], field_sem.at[k])
-        for x in group:
+        for x in groups[k]:
             for h in range(parts):
                 field_out[slot_of[x], h] = write_log(theirs_v[slot_of[x], :, plane(h)], 0)
-        if k == 0:
-            pl.semaphore_wait(barrier, greeted)
-
-            @pl.when(last_slab)
-            def _():
-                pl.semaphore_signal(seam_gate, inc=1, device_id=right, device_id_type=MESH)
-
-        if k < 2:
-            field(k).start()
-        else:
-            @pl.when(jnp.logical_not(holds_back))
-            def _(k=k):
-                field(k).start()
+
+    code_group(0)
+    pl.semaphore_wait(barrier, greeted)
+
+    @pl.when(last_slab)
+    def _():
+        pl.semaphore_signal(seam_gate, inc=1, device_id=right, device_id_type=MESH)
+
+    field(0).start()
 
     charges_copy.wait()
     q = [charges_ref[side * (NS - 2 * t) + t].astype(jnp.float32) for t in range(NS + 1)]
@@ -227,31 +222,45 @@
     taken(w_v.at[pl.ds(1, layers)], local_sem.at[0])
     taken(psi_v.at[pl.ds(2, layers)], local_sem.at[1])
     taken(start_v, local_sem.at[2])
-    for d in (0, 1):
-        edge_pair(d, make_factor)
-        edge_pair(d, functools.partial(begin_chain, OWN))
-
-        def code_edge(j, d=d):
-            x = out_layer(d, j)
+    def neighbour_of(d):
+        return (side, lax.rem(slab + slabs + 2 * d - 1, slabs))
+
+    def edge(d, k):
+        return d * (layers - 1) + k * (1 - 2 * d)
+
+    def edge_copy(n, d):
+        first, count = ((0, 4), (4, 1))[n]
+        return pltpu.make_async_remote_copy(
+            edge_out.at[d, pl.ds(first, count)], edge_in.at[d, pl.ds(first, count)],
+            edge_send, edge_recv.at[n], device_id=neighbour_of(d), device_id_type=MESH,
+        )
+
+    def code_edges(d):
+        for j in (0, 1):
+            x = edge(d, j)
+            make_factor(x)
+            begin_chain(OWN, x)
             edge_out[d, j] = write_log(u[OWN, 0, x + 2], 1)
             edge_out[d, 3 + j] = write_code(psi_v[x + 2], *psi_span)
-
-        loop(0, 2, code_edge)
-        for h in range(parts):
-            edge_out[d, 2, h] = write_code(w_v[out_layer(d, 0) + 1, :, plane(h)], *w_span)
-    edges = [
-        pltpu.make_async_remote_copy(
-            edge_out.at[d, pl.ds(first, count)], edge_in.at[d, pl.ds(first, count)],
-            edge_send, edge_recv.at[n], device_id=targets[d], device_id_type=MESH,
-        )
-        for n, (first, count) in enumerate(((0, 4), (4, 1))) for d in (0, 1)
-    ]
+        for h in range(parts):
+            edge_out[d, 2, h] = write_code(w_v[edge(d, 0) + 1, :, plane(h)], *w_span)
+
+    far = slab % 2
+    code_edges(far)
 
     @pl.when(jnp.logical_not(first_slab))
     def _():
-        edges[0].start()
-
-    edges[1].start()
+        edge_copy(0, far).start()
+
+    code_group(1)
+    field(1).start()
+    code_edges(1 - far)
+    edge_copy(0, 1 - far).start()
+    code_group(2)
+    code_group(3)
+    field(2).start()
+    field(3).start()
+
     stages = len(near)
 
     def open_gate(stage):
@@ -270,12 +279,6 @@
     adv(OWN, 1, 2, layers - 2)
     adv(OWN, 2, 3, layers - 3)
 
-    @pl.when(holds_back)
-    def _():
-        field(2).start()
-        field(3).start()
-
-
     def make_base(x):
         center, sums = around(psi_v, (x + 2,), EDGE, window.size)
         for h in range(parts):
@@ -285,16 +288,10 @@
     @pl.when(first_slab)
     def _():
         pl.semaphore_wait(seam_gate, 1)
-        edges[0].start()
+        edge_copy(0, 0).start()
 
     loop(1, layers - 1, make_base)
     pass_gate(1)
-
-    def neighbour_of(d):
-        return (side, lax.rem(slab + slabs + 2 * d - 1, slabs))
-
-    def edge(d, k):
-        return d * (layers - 1) + k * (1 - 2 * d)
 
     def halo(kind, d, first, count):
         return pltpu.make_async_remote_copy(
@@ -313,8 +310,8 @@
         for d in (0, 1):
             halo_out[0, d, j] = write_log(u[FOREIGN, 0, out_layer(d, j) + 2], 1)
             halo(0, d, j, 1).start()
-    edges[2].start()
-    edges[3].start()
+    edge_copy(1, 0).start()
+    edge_copy(1, 1).start()
 
     pass_gate(2)
     taken(edge_in.at[:, pl.ds(0, 4)], edge_recv.at[0])

time: 26.7 us -> 26.4 us (0.989)
  no operation moved by 1% of the time
where the time goes in v8:
time: 26.4 us; the launch traced here: 26.3 us
  Pallas kernels  25.7 us (97%)
  between operations  0.64 us (2%)
    pallas_call x1, Pallas kernels, body(): pl.pallas_call(functools.partial(kernel, ends, slabs), out_shape=(planes(...  24.3 us
    pallas_call x1, Pallas kernels, body(): pl.pallas_call(finishing, out_shape=(out, out), in_specs=[vmem] * 4, out_...  1.34 us

profile of v8, /device:TPU:0, one launch (start us, length us, event | category | flops | bytes accessed | tf_op | source)
XLA Modules:
  0.0 26.3 jit_solution(3954213539267476459)
XLA Ops:
  0.6 24.3 %scf_step.1 = (f32[8,2,72,128]{3,2,1,0:T(8,128)S(1)}, f32[10,2,72,128]{3,2,1,0:T(8,128)S(1)}, f32[10,2,72,128]{3,2,1,0:T(8,128)S(1)}, f32[1,128]{1,0:T(1,128)S(1)}) custom-call(s32[5]{0:T(128)} %charges_hbm.1, f32[8,128,256]{2,1,0:T(8,128)} %w_hbm.1, f32[8,128,256]{2,1,0:T(8,128)} %psi_hbm.1, f32[1,8,128,256]{3,2,1,0:T(8,128)} %start_hbm.1), custom_call_target="tpu_custom_call" | custom-call | tf_op jit(solution)/shard_map/scf_step/pallas_call | solution.py:559
  25.0 1.3 %finishing.1 = (f32[8,64,256]{2,1,0:T(8,128)}, f32[8,64,256]{2,1,0:T(8,128)}) custom-call(f32[8,2,72,128]{3,2,1,0:T(8,128)S(1)} %get-tuple-element.6.phi, f32[10,2,72,128]{3,2,1,0:T(8,128)S(1)} %get-tuple-element.7.rho, f32[10,2,72,128]{3,2,1,0:T(8,128)S(1)} %get-tuple-element.8.base, f32[1,128]{1,0:T(1,128)S(1)} %get-tuple-element.9.scale_ref), custom_call_target="tpu_custom_call" | custom-call | tf_op jit(solution)/shard_map/finishing/pallas_call | solution.py:578

commit v9 on v8

--- a/solution.py
+++ b/solution.py
@@ -232,7 +232,7 @@
         first, count = ((0, 4), (4, 1))[n]
         return pltpu.make_async_remote_copy(
             edge_out.at[d, pl.ds(first, count)], edge_in.at[d, pl.ds(first, count)],
-            edge_send, edge_recv.at[n], device_id=neighbour_of(d), device_id_type=MESH,
+            edge_send, edge_recv.at[n, d], device_id=neighbour_of(d), device_id_type=MESH,
         )
 
     def code_edges(d):
@@ -314,26 +314,21 @@
     edge_copy(1, 1).start()
 
     pass_gate(2)
-    taken(edge_in.at[:, pl.ds(0, 4)], edge_recv.at[0])
-    for d in (0, 1):
-        x = in_layer(d, 0)
-        for h in range(parts):
-            w_v[x + 1, :, plane(h)] = read_code(edge_in[d, 2, h], *w_span)
-        psi_v[x + 2] = read_code(edge_in[d, 3], *psi_span)
+    for d in (1 - far, far):
+        taken(edge_in.at[1 - d, pl.ds(0, 4)], edge_recv.at[0, 1 - d])
+        x = edge(d, -1)
+        for h in range(parts):
+            w_v[x + 1, :, plane(h)] = read_code(edge_in[1 - d, 2, h], *w_span)
+        psi_v[x + 2] = read_code(edge_in[1 - d, 3], *psi_span)
         for j in (0, 1):
-            u[OWN, 0, in_layer(d, j) + 2] = read_log(edge_in[d, j], 1)
-    beyond(make_factor)
-    beyond(functools.partial(advance_halo, OWN, 0))
-    outer(functools.partial(advance, OWN, 0))
-
-    def half_way(chain, kind):
-        for d in (0, 1):
-            edge_pair(d, functools.partial(advance, chain, 1))
-            for j in (0, 1):
-                halo_out[kind, d, j] = write_log(u[chain, 2, out_layer(d, j) + 2], 5)
-            halo(kind, d, 0, 2).start()
-
-    half_way(OWN, 1)
+            u[OWN, 0, edge(d, -1 - j) + 2] = read_log(edge_in[1 - d, j], 1)
+        make_factor(x)
+        advance_halo(OWN, 0, x)
+        advance(OWN, 0, edge(d, 0))
+        for j in (0, 1):
+            advance(OWN, 1, edge(d, j))
+            halo_out[1, d, j] = write_log(u[OWN, 2, edge(d, j) + 2], 5)
+        halo(1, d, 0, 2).start()
     arrive(2)
     ring(1, functools.partial(advance, FOREIGN, 0))
     arrive(3)
@@ -414,7 +409,8 @@
     for d in (0, 1):
         edge_pair(d, gather)
 
-    taken(edge_in.at[:, pl.ds(4, 1)], edge_recv.at[1])
+    for d in (0, 1):
+        taken(edge_in.at[d, pl.ds(4, 1)], edge_recv.at[1, d])
     for d in (0, 1):
         psi_v[in_layer(d, 1) + 2] = read_code(edge_in[d, 4], *psi_span)
     for k in (-1, 0):
@@ -567,7 +563,7 @@
             pltpu.VMEM((devices, 1, LANES), jnp.float32),
             code(layers), code(layers), code(2, 5), code(2, 5), code(3, 2, 2), code(3, 2, 2), edge_rho, edge_rho,
             pltpu.SemaphoreType.REGULAR((stages,)), pltpu.SemaphoreType.REGULAR, dma(()), dma((4,)), dma((3,)), dma(()), dma((4,)),
-            dma(()), dma((2,)), dma(()), dma((3, 2)), dma(()), dma(()), dma(()), dma(()),
+            dma(()), dma((2, 2)), dma(()), dma((3, 2)), dma(()), dma(()), dma(()), dma(()),
         ],
         compiler_params=pltpu.CompilerParams(
             collective_id=0, has_side_effects=True, vmem_limit_bytes=40 * 1024 * 1024

time: 26.4 us -> 25.9 us (0.981)
  Pallas kernels: 25.7 us -> 25.1 us
    pallas_call x1, Pallas kernels: 24.3 us -> 23.8 us  [body(): pl.pallas_call(functools.partial(kernel, ends, slabs), out_shape=(planes(...]
where the time goes in v9:
time: 25.9 us; the launch traced here: 25.8 us
  Pallas kernels  25.1 us (97%)
  between operations  0.64 us (2%)
    pallas_call x1, Pallas kernels, body(): pl.pallas_call(functools.partial(kernel, ends, slabs), out_shape=(planes(...  23.8 us
    pallas_call x1, Pallas kernels, body(): pl.pallas_call(finishing, out_shape=(out, out), in_specs=[vmem] * 4, out_...  1.34 us

profile of v9, /device:TPU:0, one launch (start us, length us, event | category | flops | bytes accessed | tf_op | source)
XLA Modules:
  0.0 25.8 jit_solution(13275870230925603646)
XLA Ops:
  0.6 23.8 %scf_step.1 = (f32[8,2,72,128]{3,2,1,0:T(8,128)S(1)}, f32[10,2,72,128]{3,2,1,0:T(8,128)S(1)}, f32[10,2,72,128]{3,2,1,0:T(8,128)S(1)}, f32[1,128]{1,0:T(1,128)S(1)}) custom-call(s32[5]{0:T(128)} %charges_hbm.1, f32[8,128,256]{2,1,0:T(8,128)} %w_hbm.1, f32[8,128,256]{2,1,0:T(8,128)} %psi_hbm.1, f32[1,8,128,256]{3,2,1,0:T(8,128)} %start_hbm.1), custom_call_target="tpu_custom_call" | custom-call | tf_op jit(solution)/shard_map/scf_step/pallas_call | solution.py:555
  24.4 1.3 %finishing.1 = (f32[8,64,256]{2,1,0:T(8,128)}, f32[8,64,256]{2,1,0:T(8,128)}) custom-call(f32[8,2,72,128]{3,2,1,0:T(8,128)S(1)} %get-tuple-element.6.phi, f32[10,2,72,128]{3,2,1,0:T(8,128)S(1)} %get-tuple-element.7.rho, f32[10,2,72,128]{3,2,1,0:T(8,128)S(1)} %get-tuple-element.8.base, f32[1,128]{1,0:T(1,128)S(1)} %get-tuple-element.9.scale_ref), custom_call_target="tpu_custom_call" | custom-call | tf_op jit(solution)/shard_map/finishing/pallas_call | solution.py:574

commit v10 on v9

--- a/solution.py
+++ b/solution.py
@@ -356,14 +356,6 @@
     adv(FOREIGN, 1, 2, layers - 2)
     adv(FOREIGN, 2, 1, layers - 1)
 
-    def second_half(chain, kind):
-        for d in (0, 1):
-            taken(halo_in.at[kind, d], halo_recv.at[kind, d])
-            for j in (0, 1):
-                u[chain, 2, in_layer(d, j) + 2] = read_log(halo_in[kind, d, j], 5)
-        beyond(functools.partial(advance_halo, chain, 2))
-        outer(functools.partial(advance, chain, 2))
-
     weights = [0.5 if t in (0, NS) else 1.0 for t in range(NS + 1)]
     charged = [weights[t] * q[t] for t in range(NS + 1)]
 
@@ -397,17 +389,20 @@
     loop(2, layers - 2, whole)
 
     pass_gate(stages - 1)
-    second_half(OWN, 1)
-    for d in (0, 1):
-        edge_pair(d, functools.partial(advance, OWN, 3))
+    for d in sides:
+        taken(halo_in.at[1, 1 - d], halo_recv.at[1, 1 - d])
+        for j in (0, 1):
+            u[OWN, 2, edge(d, -1 - j) + 2] = read_log(halo_in[1, 1 - d, j], 5)
+        advance_halo(OWN, 2, edge(d, -1))
+        advance(OWN, 2, edge(d, 0))
+        for j in (0, 1):
+            advance(OWN, 3, edge(d, j))
+            gather(edge(d, j))
 
     def cells_of(x):
         return sum(phi[x, h, inner] for h in range(parts))
 
     partial = sum(cells_of(x) for x in range(2, layers - 2))
-
-    for d in (0, 1):
-        edge_pair(d, gather)
 
     for d in (0, 1):
         taken(edge_in.at[d, pl.ds(4, 1)], edge_recv.at[1, d])

time: 25.9 us -> 25.9 us (level)
  no operation moved by 1% of the time
where the time goes in v10:
time: 25.9 us; the launch traced here: 25.8 us
  Pallas kernels  25.1 us (97%)
  between operations  0.64 us (2%)
    pallas_call x1, Pallas kernels, body(): pl.pallas_call(functools.partial(kernel, ends, slabs), out_shape=(planes(...  23.8 us
    pallas_call x1, Pallas kernels, body(): pl.pallas_call(finishing, out_shape=(out, out), in_specs=[vmem] * 4, out_...  1.34 us

profile of v10, /device:TPU:0, one launch (start us, length us, event | category | flops | bytes accessed | tf_op | source)
XLA Modules:
  0.0 25.8 jit_solution(5146855923399842198)
XLA Ops:
  0.6 23.8 %scf_step.1 = (f32[8,2,72,128]{3,2,1,0:T(8,128)S(1)}, f32[10,2,72,128]{3,2,1,0:T(8,128)S(1)}, f32[10,2,72,128]{3,2,1,0:T(8,128)S(1)}, f32[1,128]{1,0:T(1,128)S(1)}) custom-call(s32[5]{0:T(128)} %charges_hbm.1, f32[8,128,256]{2,1,0:T(8,128)} %w_hbm.1, f32[8,128,256]{2,1,0:T(8,128)} %psi_hbm.1, f32[1,8,128,256]{3,2,1,0:T(8,128)} %start_hbm.1), custom_call_target="tpu_custom_call" | custom-call | tf_op jit(solution)/shard_map/scf_step/pallas_call | solution.py:550
  24.4 1.3 %finishing.1 = (f32[8,64,256]{2,1,0:T(8,128)}, f32[8,64,256]{2,1,0:T(8,128)}) custom-call(f32[8,2,72,128]{3,2,1,0:T(8,128)S(1)} %get-tuple-element.6.phi, f32[10,2,72,128]{3,2,1,0:T(8,128)S(1)} %get-tuple-element.7.rho, f32[10,2,72,128]{3,2,1,0:T(8,128)S(1)} %get-tuple-element.8.base, f32[1,128]{1,0:T(1,128)S(1)} %get-tuple-element.9.scale_ref), custom_call_target="tpu_custom_call" | custom-call | tf_op jit(solution)/shard_map/finishing/pallas_call | solution.py:569
